TPU v7x, 32 devices: a whole 2x2x4 slice. The times are simulated.
32 devices in a mesh: dp: 8 (over y, x, core), tensor: 4 (over z).
Axes of the slice: x: 2, y: 2, z: 4, core: 2. Of those that a mesh axis runs over, the one named last changes fastest.
Arguments:
- activations: bfloat16 [4096, 8192], P('dp', 'tensor'), may hold values from -6 to 6
- out_grads: bfloat16 [4096, 28672], P('dp', 'tensor'), may hold values from -6 to 6
- input_proj: bfloat16 [8192, 64], P('tensor'), may hold values from -0.0625 to 0.0625
- grad_proj: bfloat16 [28672, 64], P('tensor'), may hold values from -4 to 4, as said below
- example_count: int32 [8], P('dp'), may hold values from 1 to 4, as said below
- child_order: int32 [8], replicated, may hold values 0 or 1
- prior_sketch: float32 [2048, 4096], P('dp', 'tensor'), may hold values from -6 to 6
- fold_map: float32 [256, 4], replicated, may hold values from -3 to 3
- merge_mix: float32 [256, 512], replicated, may hold values from -0.25 to 0.25
Outputs:
- merged_sketch: float32 [256, 4096], P(None, 'tensor')
- preconditioned: float32 [32, 4096], P('dp', 'tensor')
Inputs may be any that keep to these rules, and one draw needn't show every extreme that they name: `example_count`: some data rank has exactly 4 live examples. `grad_proj`: entries within 26 / sqrt(28672) of zero.
All inputs are finite; a program needn't handle non-finite values.
Results may differ from a plain program's by a relative error of at most 0.0003.
Values sent between devices are 32-bit elements; how exact they have to be, the bound alone decides.
A program may use at most 64 MiB of HBM per device.

v0:
```python
import functools

import jax
import jax.numpy as jnp
from jax import lax
from jax.experimental import pallas as pl
from jax.experimental.pallas import tpu as pltpu
from jax.sharding import PartitionSpec as P

RANK = 64
SEQ = 128
LANES = 128
HIGHEST = lax.Precision.HIGHEST
MESH = pl.DeviceIdType.MESH


def newton_plan(rows):
    low, high = 0.999, (rows + 1) * 1.001
    first = 2.0 / (low + high)
    reach, scales = first * low, []
    while 1.0 - reach > 1e-3:
        grown = reach * (2.0 - reach)
        scale = 2.0 / (1.0 + grown)
        scales.append(scale)
        reach = grown * scale
    return first, scales


def dot_high(left, right):
    return jnp.dot(left, right, precision=HIGHEST, preferred_element_type=jnp.float32)


def dot_flip(left, right):
    return lax.dot_general(left, right, (((1,), (1,)), ((), ())), preferred_element_type=jnp.float32)


def dot_rows(left, right):
    return lax.dot_general(
        left, right, (((1,), (1,)), ((), ())), precision=HIGHEST, preferred_element_type=jnp.float32
    )


def halves(value):
    high = value.astype(jnp.bfloat16)
    return high, (value - high.astype(jnp.float32)).astype(jnp.bfloat16)


def dot_halves(left, right):
    (a, b), (c, d) = left, right
    out = jnp.dot(a, c, preferred_element_type=jnp.float32)
    out = out + jnp.dot(a, d, preferred_element_type=jnp.float32)
    return out + jnp.dot(b, c, preferred_element_type=jnp.float32)


def dot_mid(left, right):
    return dot_halves(halves(left), halves(right))


def stacked(value, order):
    high = value.astype(jnp.bfloat16).astype(jnp.float32)
    both = (high, value - high)
    return jnp.concatenate([both[i] for i in order], axis=0)


def fused_kernel(
    n_dp,
    n_tp,
    act_hbm,
    out_hbm,
    wi_hbm,
    wo_hbm,
    count_ref,
    order_ref,
    prior_hbm,
    fold_ref,
    mix_ref,
    root_out,
    gram_out,
    rhs_out,
    grads_out,
    act,
    outg,
    wi,
    wo,
    prior,
    pair_in,
    node_send,
    node_recv,
    zsend,
    zrecv,
    full,
    grads,
    grads_by_tile,
    grads_all,
    sums_z,
    sums_p,
    root,
    gram_part,
    gram_rs,
    gram_z,
    gram,
    load_sem,
    pair_sems,
    node_sems,
    root_sems,
    z_send,
    z_recv,
    p_send,
    p_recv,
    out_sem,
):
    f32 = jnp.float32
    me, z = lax.axis_index("dp"), lax.axis_index("tensor")
    rows = gram.shape[0]
    block = rows // n_dp
    part_rows = gram_z.shape[1]
    levels = n_dp.bit_length() - 1

    def dp_of(k):
        return lax.rem(me + k, n_dp)

    def tp_of(k):
        return lax.rem(z + k, n_tp)

    order = sorted(range(1, n_tp), key=lambda k: -min(k, n_tp - k)) + [0]
    loads = []
    for index, (src, dst) in enumerate(((wi_hbm, wi), (wo_hbm, wo))):
        loads.append(pltpu.make_async_copy(src, dst, load_sem.at[index]))
        loads[-1].start()
    chunk_loads = []
    for index, k in enumerate(order):
        e = tp_of(k)
        span = pl.ds(pl.multiple_of(e * SEQ, SEQ), SEQ)
        pair = (
            pltpu.make_async_copy(act_hbm.at[span], act.at[index], load_sem.at[2 + 2 * index]),
            pltpu.make_async_copy(out_hbm.at[span], outg.at[index], load_sem.at[3 + 2 * index]),
        )
        for copy in pair:
            copy.start()
        chunk_loads.append(pair)

    def tile_of(owner):
        return pl.ds(pl.multiple_of(owner * LANES, LANES), LANES)

    own_prior = pltpu.make_async_copy(prior_hbm, prior, load_sem.at[2 + 2 * n_tp])
    own_prior.start()

    barrier = pltpu.get_barrier_semaphore()
    for k in range(1, n_dp):
        pl.semaphore_signal(barrier, inc=1, device_id={"dp": dp_of(k)}, device_id_type=MESH)
    for k in range(1, n_tp):
        pl.semaphore_signal(barrier, inc=1, device_id={"tensor": tp_of(k)}, device_id_type=MESH)
    pl.semaphore_wait(barrier, n_dp + n_tp - 2)

    half = n_dp // 2
    core, chip = lax.rem(me, 2), me // 2
    partner = me + 1 - 2 * core
    chip_x = chip + 1 - 2 * lax.rem(chip, 2)
    chip_y = chip + 2 - 4 * (chip // 2)
    chip_d = half - 1 - chip

    def push(source, target, device, sems, index):
        copy = pltpu.make_async_remote_copy(
            src_ref=source,
            dst_ref=target,
            send_sem=sems.at[0, index],
            recv_sem=sems.at[1, index],
            device_id={"dp": device},
            device_id_type=MESH,
        )
        copy.start()
        return copy

    pair_copies = [
        push(prior_hbm.at[:, tile_of(2 * q + 1 - core)], pair_in.at[q], partner, pair_sems, q)
        for q in range(half)
    ]

    def exchange(axis, phase, source, target):
        size, other = (n_tp, tp_of) if axis == "tensor" else (n_dp, dp_of)
        send, recv = (z_send, z_recv) if axis == "tensor" else (p_send, p_recv)
        copies = []
        for k in range(1, size):
            copies.append(
                pltpu.make_async_remote_copy(
                    src_ref=source(other(k)),
                    dst_ref=target,
                    send_sem=send.at[phase, k],
                    recv_sem=recv.at[phase, k],
                    device_id={axis: other(k)},
                    device_id_type=MESH,
                )
            )
            copies[-1].start()
        return copies

    for copy in loads:
        copy.wait()
    side_copies = []
    for index, k in enumerate(order):
        for copy in chunk_loads[index]:
            copy.wait()
        left = dot_flip(act[index], wi[...])
        right = dot_flip(outg[index], wo[...])
        both = jnp.concatenate([left, right], axis=1)
        if k == 0:
            zrecv[z] = both
        else:
            zsend[index] = both
            copy = pltpu.make_async_remote_copy(
                src_ref=zsend.at[index],
                dst_ref=zrecv.at[z],
                send_sem=z_send.at[0, k],
                recv_sem=z_recv.at[0, k],
                device_id={"tensor": tp_of(k)},
                device_id_type=MESH,
            )
            copy.start()
            side_copies.append(copy)

    first_mix, second_mix = mix_ref[:, :rows], mix_ref[:, rows:]
    own_prior.wait()
    for copy in pair_copies:
        copy.wait()
    own_first = order_ref[2 * chip] == core
    own_half = [prior[:, tile_of(2 * q + core)] for q in range(half)]
    firsts = [jnp.where(own_first, own_half[q], pair_in[q]) for q in range(half)]
    seconds = [jnp.where(own_first, pair_in[q], own_half[q]) for q in range(half)]
    first_halves, second_halves = halves(first_mix), halves(second_mix)
    mixed = dot_halves(first_halves, halves(jnp.concatenate(firsts, axis=1)))
    mixed = mixed + dot_halves(second_halves, halves(jnp.concatenate(seconds, axis=1)))
    for q in range(half):
        node_send[q] = mixed[:, q * LANES : (q + 1) * LANES]
    node_copies = [
        push(node_send.at[other], node_recv.at[chip], 2 * other + core, node_sems, index)
        for index, other in enumerate((chip_x, chip_y, chip_d))
    ]
    node_recv[chip] = node_send[chip]
    for copy in side_copies:
        copy.wait()
    sides = zrecv[0]
    for index in range(1, n_tp):
        sides = sides + zrecv[index]
    lane = lax.broadcasted_iota(jnp.int32, sides.shape, 1)
    doubled = jnp.where(lane < RANK, sides, pltpu.roll(sides, RANK, 1))
    product = dot_mid(sides.T, doubled) / jnp.sqrt(f32(SEQ))
    product = jnp.where(z < count_ref[0], product, jnp.zeros_like(product))
    full[...] = product[RANK:]
    even = full[pl.ds(0, RANK // 2, stride=2), :]
    odd = full[pl.ds(1, RANK // 2, stride=2), :]
    lane = lax.broadcasted_iota(jnp.int32, even.shape, 1)
    mine = jnp.where(lane < RANK, even, odd)
    for index in range(n_tp):
        zsend[n_tp + index, 0:n_dp, :] = mine[index * n_dp : (index + 1) * n_dp]
    grads[z] = zsend[n_tp + z, 0:n_dp, :]
    grad_copies = exchange("tensor", 1, lambda t: zsend.at[n_tp + t, 0:n_dp, :], grads.at[z])

    flags = [
        [order_ref[j * 2 ** (level + 1) + 2**level - 1] == 1 for j in range(n_dp >> (level + 1))]
        for level in range(levels)
    ]

    def pick(flip, lower, upper):
        first = [jnp.where(flip, b, a) for a, b in zip(lower, upper)]
        return first, [jnp.where(flip, a, b) for a, b in zip(lower, upper)]

    fold_rows = fold_ref[...]
    paths = [[jnp.concatenate([dot_rows(fold_rows, first_mix), dot_rows(fold_rows, second_mix)], axis=0)]]
    for level in range(1, levels):
        paths.append(
            [dot_rows(p, first_mix) for p in paths[-1]] + [dot_rows(p, second_mix) for p in paths[-1]]
        )
    paths = [[stacked(p, (0, 0, 1)).T.astype(jnp.bfloat16) for p in level] for level in paths]
    for copy in grad_copies:
        copy.wait()
    for index in range(n_tp):
        value = grads[index]
        for tile in range(n_dp):
            grads_by_tile[tile, index : index + 1, :] = value[tile : tile + 1]
    grads_all[me] = grads_by_tile[me]
    grad_copies = exchange("dp", 0, lambda t: grads_by_tile.at[t], grads_all.at[me])
    fold = fold_rows.T
    leaf_square = jnp.zeros((rows, LANES), f32)
    for tile in range(n_dp):
        leaf = prior[:, tile * LANES : (tile + 1) * LANES]
        step = grads_by_tile[tile]
        for e in range(n_tp):
            leaf = leaf + fold[:, e : e + 1] * step[e : e + 1, :]
        leaf_square = leaf_square + leaf * leaf

    def total(value):
        return jnp.sum(jnp.sum(value, axis=0, keepdims=True), axis=1, keepdims=True)

    own_mass = total(leaf_square)

    for copy in node_copies:
        copy.wait()
    mixtures = [[[node_recv[j]] for j in range(half)]]
    for level in range(1, levels):
        below = mixtures[-1]
        sides_of = [pick(flags[level][j], below[2 * j], below[2 * j + 1]) for j in range(len(below) // 2)]
        count = len(below[0])
        left = dot_halves(first_halves, halves(jnp.concatenate([v for f, _ in sides_of for v in f], axis=1)))
        right = dot_halves(second_halves, halves(jnp.concatenate([v for _, g in sides_of for v in g], axis=1)))
        mixtures.append(
            [
                [
                    side[:, (j * count + i) * LANES : (j * count + i + 1) * LANES]
                    for side in (left, right)
                    for i in range(count)
                ]
                for j in range(len(sides_of))
            ]
        )
    for copy in grad_copies:
        copy.wait()

    sums, products, nodes = [], [], []
    steps_of = [[grads_all[r]] for r in range(n_dp)]
    for level in range(levels):
        level_products, level_nodes, merged_steps = [], [], []
        for j in range(len(steps_of) // 2):
            first, second = pick(flags[level][j], steps_of[2 * j], steps_of[2 * j + 1])
            if level == 0:
                merged_steps.append([jnp.concatenate([first[0], second[0]], axis=0)])
            else:
                merged_steps.append(first + second)
        updates = [
            jnp.dot(
                path,
                jnp.concatenate([stacked(g[i], (0, 1, 0)) for g in merged_steps], axis=1).astype(jnp.bfloat16),
                preferred_element_type=f32,
            )
            for i, path in enumerate(paths[level])
        ]
        for j in range(len(merged_steps)):
            parts = [
                v + update[:, j * LANES : (j + 1) * LANES]
                for v, update in zip(mixtures[level][j], updates)
            ]
            index_of = {}
            for a in range(len(parts)):
                for b in range(a + 1):
                    index_of[a, b] = n_dp + len(sums)
                    sums.append(total(parts[a] * parts[b]))
            level_products.append(index_of)
            level_nodes.append(parts)
        steps_of = merged_steps
        products.append(level_products)
        nodes = level_nodes
    lane = lax.broadcasted_iota(jnp.int32, (8, LANES), 1)
    packed = jnp.where(lane == me, own_mass, jnp.zeros((8, LANES), f32))
    for index, value in enumerate(sums):
        packed = jnp.where(lane == n_dp + index, value, packed)
    sums_z[z] = packed
    for copy in exchange("tensor", 2, lambda t: sums_z.at[z], sums_z.at[z]):
        copy.wait()
    packed = sums_z[0]
    for index in range(1, n_tp):
        packed = packed + sums_z[index]
    sums_p[me] = packed
    for copy in exchange("dp", 1, lambda t: sums_p.at[me], sums_p.at[me]):
        copy.wait()
    packed = sums_p[0]
    for index in range(1, n_dp):
        packed = packed + sums_p[index]
    packed = packed[0:1]
    lane = lax.broadcasted_iota(jnp.int32, (1, LANES), 1)

    def summed(index):
        return jnp.sum(jnp.where(lane == index, packed, 0.0), axis=1, keepdims=True)

    masses = [summed(index) for index in range(n_dp)]
    scales = [[jnp.ones((1, 1), f32)] for _ in range(n_dp)]
    for level in range(levels):
        new_masses, new_scales = [], []
        for j, products_of in enumerate(products[level]):
            flip = flags[level][j]
            lower, upper = scales[2 * j], scales[2 * j + 1]
            if level == 0:
                coefs = [jnp.ones((1, 1), f32)]
            else:
                coefs = [jnp.where(flip, b, a) for a, b in zip(lower, upper)]
                coefs += [jnp.where(flip, a, b) for a, b in zip(lower, upper)]
            square = jnp.zeros((1, 1), f32)
            for (a, b), index in products_of.items():
                term = coefs[a] * (coefs[b] * summed(index))
                square = square + (term if a == b else 2.0 * term)
            mass = masses[2 * j] + masses[2 * j + 1]
            scale = jnp.sqrt(mass / (jnp.maximum(square, 0.0) + 1e-06))
            new_masses.append(mass)
            new_scales.append([scale * c for c in coefs])
        masses, scales = new_masses, new_scales
    chunk = scales[0][0] * nodes[0][0]
    for c, part in zip(scales[0][1:], nodes[0][1:]):
        chunk = chunk + c * part
    root[:, tile_of(me)] = chunk

    square_halves = halves(chunk)
    square = dot_flip(square_halves[0], square_halves[0]) + dot_flip(*square_halves)
    square = square + dot_flip(square_halves[1], square_halves[0])
    every = jnp.concatenate([grads_all[r] for r in range(n_dp)], axis=0)
    every_halves = halves(every)
    targets = dot_flip(every_halves[0], square_halves[0]) + dot_flip(every_halves[0], square_halves[1])
    targets = targets + dot_flip(every_halves[1], square_halves[0])
    filler = jnp.zeros((part_rows - block - n_tp, rows), f32)
    for r in range(n_dp):
        gram_part[r, 0:block, :] = square[r * block : (r + 1) * block]
        gram_part[r, block:, :] = jnp.concatenate([targets[r * n_tp : (r + 1) * n_tp], filler], axis=0)
    gram_rs[me] = gram_part[me]
    gram_copies = exchange("dp", 2, lambda t: gram_part.at[t], gram_rs.at[me])
    dev_x, dev_y, dev_d = (2 * other + core for other in (chip_x, chip_y, chip_d))
    upper, lower = pl.ds(0, rows // 2), pl.ds(rows // 2, rows // 2)

    def relay(index, owner, device, span=slice(None)):
        block_of = root.at[span, tile_of(owner)]
        return push(block_of, block_of, device, root_sems, index)

    relays = [relay(0, me, dev_x), relay(1, me, dev_y), relay(2, me, partner)]
    for index in range(n_tp):
        value = grads[index]
        for tile in range(n_dp):
            grads_out[index : index + 1, tile * LANES : (tile + 1) * LANES] = value[tile : tile + 1]
    for copy in gram_copies:
        copy.wait()
    part = gram_rs[0]
    for index in range(1, n_dp):
        part = part + gram_rs[index]
    gram_z[z] = part
    z_copies = exchange("tensor", 3, lambda t: gram_z.at[z], gram_z.at[z])
    relays[0].wait_recv()
    relays.append(relay(3, dev_x, dev_y, upper))
    relays.append(relay(4, dev_x, partner))
    relays[1].wait_recv()
    relays.append(relay(5, dev_y, dev_x, lower))
    relays.append(relay(6, dev_y, partner))
    for copy in z_copies:
        copy.wait()
    part = gram_z[0]
    for index in range(1, n_tp):
        part = part + gram_z[index]
    own_rows = pl.ds(pl.multiple_of(me * block, block), block)
    gram[own_rows, :] = part[0:block]
    gram_copies = exchange("dp", 4, lambda t: gram.at[own_rows], gram.at[own_rows])
    rhs_out[...] = part[block : block + n_tp]
    relays[3].wait_recv()
    relays[5].wait_recv()
    relays.append(relay(7, dev_d, partner))
    for index, copy in enumerate(relays):
        copy.wait_send()
        if index not in (0, 1, 3, 5):
            copy.wait_recv()
    root_write = pltpu.make_async_copy(root, root_out, out_sem.at[0])
    root_write.start()
    for copy in gram_copies:
        copy.wait()
    gram_out[...] = gram[...]
    root_write.wait()


def solve_kernel(root_hbm, gram_ref, rhs_ref, grads_ref, root_out, pre_out, root, sems):
    read = pltpu.make_async_copy(root_hbm, root, sems.at[0])
    read.start()
    system = gram_ref[...]
    rows = system.shape[0]
    eye = lax.broadcasted_iota(jnp.int32, system.shape, 0) == lax.broadcasted_iota(
        jnp.int32, system.shape, 1
    )
    trace = jnp.sum(
        jnp.sum(jnp.where(eye, system, 0.0), axis=0, keepdims=True), axis=1, keepdims=True
    )
    unit = 1.0 / (trace / rows)
    system = system * unit + jnp.where(eye, 1.0, 0.0)
    system_halves = halves(system)
    first, steps = newton_plan(rows)
    inverse = jnp.where(eye, 2.0 * first * steps[0], 0.0) - (first * first * steps[0]) * system
    for scale in steps[1:]:
        inverse_halves = halves(inverse)
        residual = jnp.where(eye, 2.0, 0.0) - dot_halves(system_halves, inverse_halves)
        inverse = scale * dot_halves(inverse_halves, halves(residual))
    read.wait()
    write = pltpu.make_async_copy(root, root_out, sems.at[1])
    write.start()
    target = rhs_ref[...] * unit
    inverse_halves = halves(inverse)
    solved = dot_halves(halves(target), inverse_halves)
    for _ in range(2):
        solved = solved + dot_halves(halves(target - dot_high(solved, system)), inverse_halves)
    pre_out[...] = grads_ref[...] - dot_mid(solved, root[...])
    write.wait()


def fused_body(
    activations,
    out_grads,
    input_proj,
    grad_proj,
    example_count,
    child_order,
    prior_sketch,
    fold_map,
    merge_mix,
):
    n_dp, n_tp = lax.axis_size("dp"), lax.axis_size("tensor")
    rows, columns = prior_sketch.shape
    slots = activations.shape[0] // SEQ
    f32, bf16 = jnp.float32, jnp.bfloat16
    width, hidden = activations.shape[1], out_grads.shape[1]
    phases = 5
    hbm = pl.BlockSpec(memory_space=pl.ANY)
    vmem = pl.BlockSpec(memory_space=pltpu.VMEM)
    smem = pl.BlockSpec(memory_space=pltpu.SMEM)
    part_rows = -(-(rows // n_dp + slots) // 8) * 8
    root, gram, rhs, grads = pl.pallas_call(
        functools.partial(fused_kernel, n_dp, n_tp),
        out_shape=(
            jax.ShapeDtypeStruct((rows, columns), f32),
            jax.ShapeDtypeStruct((rows, rows), f32),
            jax.ShapeDtypeStruct((slots, rows), f32),
            jax.ShapeDtypeStruct((slots, columns), f32),
        ),
        in_specs=[hbm, hbm, hbm, hbm, smem, smem, hbm, vmem, vmem],
        out_specs=(hbm, vmem, vmem, vmem),
        scratch_shapes=[
            pltpu.VMEM((slots, SEQ, width), bf16),
            pltpu.VMEM((slots, SEQ, hidden), bf16),
            pltpu.VMEM((RANK, width), bf16),
            pltpu.VMEM((RANK, hidden), bf16),
            pltpu.VMEM((rows, columns), f32),
            pltpu.VMEM((n_dp // 2, rows, LANES), f32),
            pltpu.VMEM((n_dp // 2, rows, LANES), f32),
            pltpu.VMEM((n_dp // 2, rows, LANES), f32),
            pltpu.VMEM((2 * n_tp, SEQ, LANES), f32),
            pltpu.VMEM((n_tp, SEQ, LANES), f32),
            pltpu.VMEM((RANK, LANES), f32),
            pltpu.VMEM((n_tp, n_dp, LANES), f32),
            pltpu.VMEM((n_dp, n_tp, LANES), f32),
            pltpu.VMEM((n_dp, n_tp, LANES), f32),
            pltpu.VMEM((n_tp, 8, LANES), f32),
            pltpu.VMEM((n_dp, 8, LANES), f32),
            pltpu.VMEM((rows, columns), f32),
            pltpu.VMEM((n_dp, part_rows, rows), f32),
            pltpu.VMEM((n_dp, part_rows, rows), f32),
            pltpu.VMEM((n_tp, part_rows, rows), f32),
            pltpu.VMEM((rows, rows), f32),
            pltpu.SemaphoreType.DMA((3 + 2 * n_tp,)),
            pltpu.SemaphoreType.DMA((2, n_dp // 2)),
            pltpu.SemaphoreType.DMA((2, 3)),
            pltpu.SemaphoreType.DMA((2, 8)),
            pltpu.SemaphoreType.DMA((phases, n_tp)),
            pltpu.SemaphoreType.DMA((phases, n_tp)),
            pltpu.SemaphoreType.DMA((phases, n_dp)),
            pltpu.SemaphoreType.DMA((phases, n_dp)),
            pltpu.SemaphoreType.DMA((1,)),
        ],
        compiler_params=pltpu.CompilerParams(
            collective_id=0, has_side_effects=True, vmem_limit_bytes=56 * 2**20
        ),
    )(
        activations,
        out_grads,
        input_proj.T,
        grad_proj.T,
        example_count,
        child_order,
        prior_sketch,
        fold_map.T,
        merge_mix,
    )
    return pl.pallas_call(
        solve_kernel,
        out_shape=(
            jax.ShapeDtypeStruct((rows, columns), f32),
            jax.ShapeDtypeStruct((slots, columns), f32),
        ),
        in_specs=[hbm, vmem, vmem, vmem],
        out_specs=(hbm, vmem),
        scratch_shapes=[pltpu.VMEM((rows, columns), f32), pltpu.SemaphoreType.DMA((2,))],
        compiler_params=pltpu.CompilerParams(vmem_limit_bytes=56 * 2**20),
    )(root, gram, rhs, grads)


def from_partner(value, axis, stride):
    mask = 2**stride
    pairs = [(source, source ^ mask) for source in range(lax.axis_size(axis))]
    return lax.ppermute(value, axis, pairs)


def body(
    activations,
    out_grads,
    input_proj,
    grad_proj,
    example_count,
    child_order,
    prior_sketch,
    fold_map,
    merge_mix,
):
    tensor_count = lax.axis_size("tensor")
    own_rank = RANK // tensor_count
    example_slots = activations.shape[0] // SEQ
    sketch_rows = prior_sketch.shape[0]
    input_part = jnp.dot(activations, input_proj, preferred_element_type=jnp.float32)
    grad_part = jnp.dot(out_grads, grad_proj, preferred_element_type=jnp.float32)
    input_side, grad_side = lax.psum((input_part, grad_part), "tensor")
    grad_own = lax.dynamic_slice_in_dim(grad_side, lax.axis_index("tensor") * own_rank, own_rank, 1)
    grad_blocks = grad_own.reshape(example_slots, SEQ, own_rank)
    input_blocks = input_side.reshape(example_slots, SEQ, RANK)
    example_grad = jnp.einsum(
        "eta,etb->eab", grad_blocks, input_blocks, precision=lax.Precision.HIGHEST
    )
    example_grad = example_grad.reshape(example_slots, own_rank * RANK) / jnp.sqrt(jnp.float32(SEQ))
    live = jnp.arange(example_slots, dtype=jnp.int32) < example_count[0]
    example_grad = jnp.where(live[:, None], example_grad, jnp.zeros_like(example_grad))
    leaf_node = prior_sketch + jnp.dot(fold_map, example_grad, precision=lax.Precision.HIGHEST)
    leaf_weight = lax.psum(jnp.sum(leaf_node * leaf_node), "tensor")
    mix_first = merge_mix[:, :sketch_rows]
    mix_second = merge_mix[:, sketch_rows:]
    depth_count = lax.axis_size("dp").bit_length() - 1
    rank_index = lax.axis_index("dp")
    sketch_node = leaf_node
    sketch_weight = leaf_weight
    for level_index in range(depth_count):
        sibling_node, sibling_weight = from_partner((sketch_node, sketch_weight), "dp", level_index)
        upper_half = rank_index >> level_index & 1
        block_start = rank_index >> level_index + 1 << level_index + 1
        flip_order = child_order[block_start + (1 << level_index) - 1]
        own_first = upper_half == flip_order
        first = jnp.where(own_first, sketch_node, sibling_node)
        second = jnp.where(own_first, sibling_node, sketch_node)
        first_weight = jnp.where(own_first, sketch_weight, sibling_weight)
        second_weight = jnp.where(own_first, sibling_weight, sketch_weight)
        mixture = jnp.dot(mix_first, first, precision=lax.Precision.HIGHEST) + jnp.dot(
            mix_second, second, precision=lax.Precision.HIGHEST
        )
        mix_total = lax.psum(jnp.sum(mixture * mixture), "tensor")
        sketch_weight = first_weight + second_weight
        sketch_node = mixture * jnp.sqrt(sketch_weight / (mix_total + 1e-06))
    gram_part = jnp.dot(sketch_node, sketch_node.T, precision=lax.Precision.HIGHEST)
    product_part = jnp.dot(sketch_node, example_grad.T, precision=lax.Precision.HIGHEST)
    gram, sketch_grad = lax.psum((gram_part, product_part), "tensor")
    damping = jnp.trace(gram) / sketch_rows
    system = gram + damping * jnp.eye(sketch_rows, dtype=jnp.float32)
    factor = jnp.linalg.cholesky(system)
    solved = jax.scipy.linalg.cho_solve((factor, True), sketch_grad)
    preconditioned = example_grad - jnp.dot(solved.T, sketch_node, precision=lax.Precision.HIGHEST)
    return (sketch_node, preconditioned)


def fits_fused(rows, columns, slots, n_dp, n_tp):
    return (
        columns == n_dp * LANES
        and slots == n_tp
        and 2 * RANK == LANES
        and n_dp == 8
        and rows % (8 * n_dp) == 0
    )


def step(*args):
    n_dp, n_tp = lax.axis_size("dp"), lax.axis_size("tensor")
    slots = args[0].shape[0] // SEQ
    rows, columns = args[6].shape
    if fits_fused(rows, columns, slots, n_dp, n_tp):
        return fused_body(*args)
    return body(*args)


def solution(mesh):
    in_specs = (
        P("dp", "tensor"),
        P("dp", "tensor"),
        P("tensor", None),
        P("tensor", None),
        P("dp"),
        P(),
        P("dp", "tensor"),
        P(),
        P(),
    )
    out_specs = (P(None, "tensor"), P("dp", "tensor"))
    return jax.shard_map(step, mesh=mesh, in_specs=in_specs, out_specs=out_specs, check_vma=False)
```

profile of v0, /device:TPU:0, one launch (start us, length us, event | category | flops | bytes accessed | tf_op | source)
XLA Modules:
  0.0 54.5 jit_solution(9177496844120128206)
XLA Ops:
  1.3 46.7 %shard_map.104 = (f32[256,1024]{1,0:T(8,128)}, f32[256,256]{1,0:T(8,128)}, f32[4,256]{1,0:T(4,128)}, f32[4,1024]{1,0:T(4,128)}) custom-call(bf16[512,2048]{1,0:T(8,128)(2,1)} %act_hbm.1, bf16[512,7168]{1,0:T(8,128)(2,1)} %out_hbm.1, bf16[64,2048]{1,0:T(8,128)(2,1)} %bitcast.4, bf16[64,7168]{1,0:T(8,128)(2,1)} %bitcast.3, s32[1]{0:T(128)S(6)} %copy.11.count_ref, ...), custom_call_target="tpu_custom_call" | custom-call | tf_op jit(solution)/shard_map/pallas_call | solution.py:514
  48.0 6.5 %shard_map.105 = (f32[256,1024]{1,0:T(8,128)}, f32[4,1024]{1,0:T(4,128)}) custom-call(f32[256,1024]{1,0:T(8,128)} %get-tuple-element.6.root_hbm, f32[256,256]{1,0:T(8,128)} %get-tuple-element.7.gram_ref, f32[4,256]{1,0:T(4,128)} %get-tuple-element.8.rhs_ref, f32[4,1024]{1,0:T(4,128)} %get-tuple-element.9.grads_ref), custom_call_target="tpu_custom_call" | custom-call | tf_op jit(solution)/shard_map/pallas_call | solution.py:570
where the time goes:
time: 54.7 us; the launch traced here: 54.5 us
  Pallas kernels  53.2 us (97%)
  between operations  1.29 us (2%)
    pallas_call x1, Pallas kernels, fused_body(): pl.pallas_call(functools.partial(fused_kernel, n_dp, n_tp), out_shape=(ja...  46.7 us
    pallas_call x1, Pallas kernels, fused_body(): pl.pallas_call(solve_kernel, out_shape=(jax.ShapeDtypeStruct((rows, colum...  6.51 us

commit v1 on v0

--- a/solution.py
+++ b/solution.py
@@ -56,10 +56,59 @@
     return dot_halves(halves(left), halves(right))
 
 
+def dot_flip_halves(left, right):
+    (a, b), (c, d) = left, right
+    return dot_flip(jnp.concatenate([a, a, b], axis=1), jnp.concatenate([c, d, c], axis=1))
+
+
+def dot_split(left, right):
+    (a, b), (c, d) = left, right
+    half = a.shape[1] // 2
+    first = jnp.dot(
+        jnp.concatenate([a, b[:, :half]], axis=1),
+        jnp.concatenate([c, c[:half]], axis=0),
+        preferred_element_type=jnp.float32,
+    )
+    second = jnp.dot(
+        jnp.concatenate([a, b[:, half:]], axis=1),
+        jnp.concatenate([d, c[half:]], axis=0),
+        preferred_element_type=jnp.float32,
+    )
+    return first + second
+
+
 def stacked(value, order):
     high = value.astype(jnp.bfloat16).astype(jnp.float32)
     both = (high, value - high)
     return jnp.concatenate([both[i] for i in order], axis=0)
+
+
+def solve(gram, target):
+    rows = gram.shape[0]
+    eye = lax.broadcasted_iota(jnp.int32, gram.shape, 0) == lax.broadcasted_iota(jnp.int32, gram.shape, 1)
+    trace = jnp.sum(
+        jnp.sum(jnp.where(eye, gram, 0.0), axis=0, keepdims=True), axis=1, keepdims=True
+    )
+    unit = 1.0 / (trace / rows)
+    system = gram * unit + jnp.where(eye, 1.0, 0.0)
+    target = target * unit
+    first, scales = newton_plan(rows)
+    state, solved, path = first * system, first * target, None
+    for index, scale in enumerate(scales):
+        factor = jnp.where(eye, 2.0 * scale, 0.0) - scale * state
+        factor_halves = halves(factor)
+        solved = dot_split(halves(solved), factor_halves)
+        if index < len(scales) - 1:
+            state = dot_split(halves(state), factor_halves)
+            if path is None:
+                path = factor_halves[0]
+            else:
+                path = jnp.dot(path, factor_halves[0], preferred_element_type=jnp.float32)
+                path = path.astype(jnp.bfloat16)
+    high, low = halves(first * (target - dot_high(solved, system)))
+    step = jnp.dot(high, path, preferred_element_type=jnp.float32)
+    step = step + jnp.dot(low, path, preferred_element_type=jnp.float32)
+    return solved + dot_split(halves(step), factor_halves)
 
 
 def fused_kernel(
@@ -72,17 +121,18 @@
     count_ref,
     order_ref,
     prior_hbm,
-    fold_ref,
-    mix_ref,
+    fold_hbm,
+    mix_hbm,
     root_out,
-    gram_out,
-    rhs_out,
+    solved_out,
     grads_out,
     act,
     outg,
     wi,
     wo,
     prior,
+    fold_ref,
+    mix_ref,
     pair_in,
     node_send,
     node_recv,
@@ -90,15 +140,14 @@
     zrecv,
     full,
     grads,
-    grads_by_tile,
+    grads_rows,
     grads_all,
-    sums_z,
-    sums_p,
+    sums_all,
     root,
     gram_part,
     gram_rs,
     gram_z,
-    gram,
+    gram_all,
     load_sem,
     pair_sems,
     node_sems,
@@ -107,12 +156,14 @@
     z_recv,
     p_send,
     p_recv,
+    a_send,
+    a_recv,
     out_sem,
+    ready_sem,
 ):
     f32 = jnp.float32
     me, z = lax.axis_index("dp"), lax.axis_index("tensor")
-    rows = gram.shape[0]
-    block = rows // n_dp
+    rows = prior.shape[0]
     part_rows = gram_z.shape[1]
     levels = n_dp.bit_length() - 1
 
@@ -124,33 +175,35 @@
 
     order = sorted(range(1, n_tp), key=lambda k: -min(k, n_tp - k)) + [0]
     loads = []
-    for index, (src, dst) in enumerate(((wi_hbm, wi), (wo_hbm, wo))):
-        loads.append(pltpu.make_async_copy(src, dst, load_sem.at[index]))
-        loads[-1].start()
-    chunk_loads = []
-    for index, k in enumerate(order):
-        e = tp_of(k)
-        span = pl.ds(pl.multiple_of(e * SEQ, SEQ), SEQ)
-        pair = (
-            pltpu.make_async_copy(act_hbm.at[span], act.at[index], load_sem.at[2 + 2 * index]),
-            pltpu.make_async_copy(out_hbm.at[span], outg.at[index], load_sem.at[3 + 2 * index]),
-        )
-        for copy in pair:
-            copy.start()
-        chunk_loads.append(pair)
+
+    def load(source, target):
+        copy = pltpu.make_async_copy(source, target, load_sem.at[len(loads)])
+        copy.start()
+        loads.append(copy)
+        return copy
+
+    def load_chunk(index):
+        span = pl.ds(pl.multiple_of(tp_of(order[index]) * SEQ, SEQ), SEQ)
+        return load(act_hbm.at[span], act.at[index]), load(out_hbm.at[span], outg.at[index])
+
+    weight_loads = [load(wi_hbm, wi), load(wo_hbm, wo)]
+    chunk_loads = [load_chunk(0)]
+    own_prior = load(prior_hbm, prior)
+    mix_load = load(mix_hbm, mix_ref)
+    chunk_loads += [load_chunk(index) for index in range(1, n_tp)]
+    fold_load = load(fold_hbm, fold_ref)
 
     def tile_of(owner):
         return pl.ds(pl.multiple_of(owner * LANES, LANES), LANES)
 
-    own_prior = pltpu.make_async_copy(prior_hbm, prior, load_sem.at[2 + 2 * n_tp])
-    own_prior.start()
-
     barrier = pltpu.get_barrier_semaphore()
+    for k in range(1, n_tp):
+        pl.semaphore_signal(barrier, inc=1, device_id={"tensor": tp_of(k)}, device_id_type=MESH)
     for k in range(1, n_dp):
         pl.semaphore_signal(barrier, inc=1, device_id={"dp": dp_of(k)}, device_id_type=MESH)
-    for k in range(1, n_tp):
-        pl.semaphore_signal(barrier, inc=1, device_id={"tensor": tp_of(k)}, device_id_type=MESH)
     pl.semaphore_wait(barrier, n_dp + n_tp - 2)
+    for k in range(1, n_dp):
+        pl.semaphore_signal(ready_sem, inc=1, device_id={"dp": dp_of(k)}, device_id_type=MESH)
 
     half = n_dp // 2
     core, chip = lax.rem(me, 2), me // 2
@@ -194,34 +247,59 @@
             copies[-1].start()
         return copies
 
-    for copy in loads:
-        copy.wait()
+    def exchange_all(phase, source, target):
+        copies = []
+        for j in sorted(range(n_tp), key=lambda j: -min(j, n_tp - j)):
+            for k in range(n_dp):
+                if j == 0 and k == 0:
+                    continue
+                copies.append(
+                    pltpu.make_async_remote_copy(
+                        src_ref=source(dp_of(k), tp_of(j)),
+                        dst_ref=target,
+                        send_sem=a_send.at[phase, j * n_dp + k],
+                        recv_sem=a_recv.at[phase, j * n_dp + k],
+                        device_id={"dp": dp_of(k), "tensor": tp_of(j)},
+                        device_id_type=MESH,
+                    )
+                )
+                copies[-1].start()
+        return copies
+
     side_copies = []
-    for index, k in enumerate(order):
+
+    def do_chunk(index):
+        k = order[index]
         for copy in chunk_loads[index]:
             copy.wait()
-        left = dot_flip(act[index], wi[...])
-        right = dot_flip(outg[index], wo[...])
-        both = jnp.concatenate([left, right], axis=1)
+        mid = SEQ // 2
+        right = [dot_flip(outg[index, h * mid : (h + 1) * mid], wo[...]) for h in range(2)]
+        left = [dot_flip(act[index, h * mid : (h + 1) * mid], wi[...]) for h in range(2)]
+        both = jnp.concatenate([jnp.concatenate(pair, axis=1) for pair in zip(left, right)], axis=0)
         if k == 0:
             zrecv[z] = both
-        else:
-            zsend[index] = both
-            copy = pltpu.make_async_remote_copy(
-                src_ref=zsend.at[index],
-                dst_ref=zrecv.at[z],
-                send_sem=z_send.at[0, k],
-                recv_sem=z_recv.at[0, k],
-                device_id={"tensor": tp_of(k)},
-                device_id_type=MESH,
-            )
-            copy.start()
-            side_copies.append(copy)
-
+            return
+        zsend[index] = both
+        copy = pltpu.make_async_remote_copy(
+            src_ref=zsend.at[index],
+            dst_ref=zrecv.at[z],
+            send_sem=z_send.at[0, k],
+            recv_sem=z_recv.at[0, k],
+            device_id={"tensor": tp_of(k)},
+            device_id_type=MESH,
+        )
+        copy.start()
+        side_copies.append(copy)
+
+    for copy in weight_loads:
+        copy.wait()
+    do_chunk(0)
+
+    own_prior.wait()
+    mix_load.wait()
+    for copy in pair_copies:
+        copy.wait()
     first_mix, second_mix = mix_ref[:, :rows], mix_ref[:, rows:]
-    own_prior.wait()
-    for copy in pair_copies:
-        copy.wait()
     own_first = order_ref[2 * chip] == core
     own_half = [prior[:, tile_of(2 * q + core)] for q in range(half)]
     firsts = [jnp.where(own_first, own_half[q], pair_in[q]) for q in range(half)]
@@ -236,6 +314,19 @@
         for index, other in enumerate((chip_x, chip_y, chip_d))
     ]
     node_recv[chip] = node_send[chip]
+    for index in range(1, n_tp):
+        do_chunk(index)
+
+    fold_load.wait()
+    fold_rows = fold_ref[...]
+    paths = [[jnp.concatenate([dot_rows(fold_rows, first_mix), dot_rows(fold_rows, second_mix)], axis=0)]]
+    for level in range(1, levels):
+        paths.append(
+            [dot_rows(p, first_mix) for p in paths[-1]] + [dot_rows(p, second_mix) for p in paths[-1]]
+        )
+    paths = [[stacked(p, (0, 0, 1)).T.astype(jnp.bfloat16) for p in level] for level in paths]
+    fold = fold_rows.T
+
     for copy in side_copies:
         copy.wait()
     sides = zrecv[0]
@@ -250,10 +341,16 @@
     odd = full[pl.ds(1, RANK // 2, stride=2), :]
     lane = lax.broadcasted_iota(jnp.int32, even.shape, 1)
     mine = jnp.where(lane < RANK, even, odd)
+    for row in range(n_tp * n_dp):
+        grads_rows[row] = mine[row : row + 1]
     for index in range(n_tp):
         zsend[n_tp + index, 0:n_dp, :] = mine[index * n_dp : (index + 1) * n_dp]
     grads[z] = zsend[n_tp + z, 0:n_dp, :]
+    slot = me * n_tp + z
+    grads_all[slot] = grads_rows[z * n_dp + me]
+    pl.semaphore_wait(ready_sem, n_dp - 1)
     grad_copies = exchange("tensor", 1, lambda t: zsend.at[n_tp + t, 0:n_dp, :], grads.at[z])
+    row_copies = exchange_all(0, lambda d, t: grads_rows.at[t * n_dp + d], grads_all.at[slot])
 
     flags = [
         [order_ref[j * 2 ** (level + 1) + 2**level - 1] == 1 for j in range(n_dp >> (level + 1))]
@@ -264,34 +361,8 @@
         first = [jnp.where(flip, b, a) for a, b in zip(lower, upper)]
         return first, [jnp.where(flip, a, b) for a, b in zip(lower, upper)]
 
-    fold_rows = fold_ref[...]
-    paths = [[jnp.concatenate([dot_rows(fold_rows, first_mix), dot_rows(fold_rows, second_mix)], axis=0)]]
-    for level in range(1, levels):
-        paths.append(
-            [dot_rows(p, first_mix) for p in paths[-1]] + [dot_rows(p, second_mix) for p in paths[-1]]
-        )
-    paths = [[stacked(p, (0, 0, 1)).T.astype(jnp.bfloat16) for p in level] for level in paths]
-    for copy in grad_copies:
-        copy.wait()
-    for index in range(n_tp):
-        value = grads[index]
-        for tile in range(n_dp):
-            grads_by_tile[tile, index : index + 1, :] = value[tile : tile + 1]
-    grads_all[me] = grads_by_tile[me]
-    grad_copies = exchange("dp", 0, lambda t: grads_by_tile.at[t], grads_all.at[me])
-    fold = fold_rows.T
-    leaf_square = jnp.zeros((rows, LANES), f32)
-    for tile in range(n_dp):
-        leaf = prior[:, tile * LANES : (tile + 1) * LANES]
-        step = grads_by_tile[tile]
-        for e in range(n_tp):
-            leaf = leaf + fold[:, e : e + 1] * step[e : e + 1, :]
-        leaf_square = leaf_square + leaf * leaf
-
     def total(value):
         return jnp.sum(jnp.sum(value, axis=0, keepdims=True), axis=1, keepdims=True)
-
-    own_mass = total(leaf_square)
 
     for copy in node_copies:
         copy.wait()
@@ -312,11 +383,27 @@
                 for j in range(len(sides_of))
             ]
         )
+
     for copy in grad_copies:
         copy.wait()
-
+    leaf_square = jnp.zeros((rows, LANES), f32)
+    for tile in range(n_dp):
+        leaf = prior[:, tile * LANES : (tile + 1) * LANES]
+        for e in range(n_tp):
+            step = grads[e, tile : tile + 1, :]
+            grads_out[e : e + 1, tile * LANES : (tile + 1) * LANES] = step
+            leaf = leaf + fold[:, e : e + 1] * step
+        leaf_square = leaf_square + leaf * leaf
+    own_mass = total(leaf_square)
+
+    for copy in row_copies:
+        copy.wait()
+    steps_of = [
+        [jnp.concatenate([grads_all[r * n_tp + e] for e in range(n_tp)], axis=0)] for r in range(n_dp)
+    ]
+    every = jnp.concatenate([step[0] for step in steps_of], axis=0)
+    every_halves = halves(every)
     sums, products, nodes = [], [], []
-    steps_of = [[grads_all[r]] for r in range(n_dp)]
     for level in range(levels):
         level_products, level_nodes, merged_steps = [], [], []
         for j in range(len(steps_of) // 2):
@@ -348,24 +435,17 @@
         steps_of = merged_steps
         products.append(level_products)
         nodes = level_nodes
-    lane = lax.broadcasted_iota(jnp.int32, (8, LANES), 1)
-    packed = jnp.where(lane == me, own_mass, jnp.zeros((8, LANES), f32))
+    lane = lax.broadcasted_iota(jnp.int32, (1, LANES), 1)
+    packed = jnp.where(lane == me, own_mass, jnp.zeros((1, LANES), f32))
     for index, value in enumerate(sums):
         packed = jnp.where(lane == n_dp + index, value, packed)
-    sums_z[z] = packed
-    for copy in exchange("tensor", 2, lambda t: sums_z.at[z], sums_z.at[z]):
-        copy.wait()
-    packed = sums_z[0]
-    for index in range(1, n_tp):
-        packed = packed + sums_z[index]
-    sums_p[me] = packed
-    for copy in exchange("dp", 1, lambda t: sums_p.at[me], sums_p.at[me]):
-        copy.wait()
-    packed = sums_p[0]
-    for index in range(1, n_dp):
-        packed = packed + sums_p[index]
-    packed = packed[0:1]
-    lane = lax.broadcasted_iota(jnp.int32, (1, LANES), 1)
+    sums_all[slot] = packed
+    for copy in exchange_all(1, lambda d, t: sums_all.at[slot], sums_all.at[slot]):
+        copy.wait()
+    parts_of = [sums_all[index] for index in range(n_tp * n_dp)]
+    while len(parts_of) > 1:
+        parts_of = [a + b for a, b in zip(parts_of[0::2], parts_of[1::2])]
+    packed = parts_of[0]
 
     def summed(index):
         return jnp.sum(jnp.where(lane == index, packed, 0.0), axis=1, keepdims=True)
@@ -396,19 +476,22 @@
         chunk = chunk + c * part
     root[:, tile_of(me)] = chunk
 
-    square_halves = halves(chunk)
-    square = dot_flip(square_halves[0], square_halves[0]) + dot_flip(*square_halves)
-    square = square + dot_flip(square_halves[1], square_halves[0])
-    every = jnp.concatenate([grads_all[r] for r in range(n_dp)], axis=0)
-    every_halves = halves(every)
-    targets = dot_flip(every_halves[0], square_halves[0]) + dot_flip(every_halves[0], square_halves[1])
-    targets = targets + dot_flip(every_halves[1], square_halves[0])
-    filler = jnp.zeros((part_rows - block - n_tp, rows), f32)
+    chunk_halves = halves(chunk)
+    upper_halves, lower_halves = [[v[s] for v in chunk_halves] for s in (slice(0, LANES), slice(LANES, rows))]
+    targets = dot_flip_halves(every_halves, chunk_halves)
+    triangle = jnp.concatenate(
+        [
+            dot_flip_halves(chunk_halves, upper_halves),
+            dot_flip_halves(lower_halves, lower_halves),
+            targets[:, :LANES],
+            targets[:, LANES:],
+        ],
+        axis=0,
+    )
     for r in range(n_dp):
-        gram_part[r, 0:block, :] = square[r * block : (r + 1) * block]
-        gram_part[r, block:, :] = jnp.concatenate([targets[r * n_tp : (r + 1) * n_tp], filler], axis=0)
+        gram_part[r] = triangle[r * part_rows : (r + 1) * part_rows]
     gram_rs[me] = gram_part[me]
-    gram_copies = exchange("dp", 2, lambda t: gram_part.at[t], gram_rs.at[me])
+    gram_copies = exchange("dp", 0, lambda t: gram_part.at[t], gram_rs.at[me])
     dev_x, dev_y, dev_d = (2 * other + core for other in (chip_x, chip_y, chip_d))
     upper, lower = pl.ds(0, rows // 2), pl.ds(rows // 2, rows // 2)
 
@@ -417,17 +500,13 @@
         return push(block_of, block_of, device, root_sems, index)
 
     relays = [relay(0, me, dev_x), relay(1, me, dev_y), relay(2, me, partner)]
-    for index in range(n_tp):
-        value = grads[index]
-        for tile in range(n_dp):
-            grads_out[index : index + 1, tile * LANES : (tile + 1) * LANES] = value[tile : tile + 1]
     for copy in gram_copies:
         copy.wait()
     part = gram_rs[0]
     for index in range(1, n_dp):
         part = part + gram_rs[index]
     gram_z[z] = part
-    z_copies = exchange("tensor", 3, lambda t: gram_z.at[z], gram_z.at[z])
+    z_copies = exchange("tensor", 2, lambda t: gram_z.at[z], gram_z.at[z])
     relays[0].wait_recv()
     relays.append(relay(3, dev_x, dev_y, upper))
     relays.append(relay(4, dev_x, partner))
@@ -439,54 +518,42 @@
     part = gram_z[0]
     for index in range(1, n_tp):
         part = part + gram_z[index]
-    own_rows = pl.ds(pl.multiple_of(me * block, block), block)
-    gram[own_rows, :] = part[0:block]
-    gram_copies = exchange("dp", 4, lambda t: gram.at[own_rows], gram.at[own_rows])
-    rhs_out[...] = part[block : block + n_tp]
+    gram_all[me] = part
+    gram_copies = exchange("dp", 1, lambda t: gram_all.at[me], gram_all.at[me])
     relays[3].wait_recv()
     relays[5].wait_recv()
     relays.append(relay(7, dev_d, partner))
+    for copy in gram_copies:
+        copy.wait()
+    triangle = jnp.concatenate([gram_all[r] for r in range(n_dp)], axis=0)
+    corner = triangle[LANES:rows]
+    gram = jnp.concatenate(
+        [
+            jnp.concatenate([triangle[:LANES], corner.T], axis=1),
+            jnp.concatenate([corner, triangle[rows : rows + LANES]], axis=1),
+        ],
+        axis=0,
+    )
+    targets = triangle[rows + LANES :]
+    target = jnp.zeros((n_tp, rows), f32)
+    for r in range(n_dp):
+        span = slice(r * n_tp, (r + 1) * n_tp)
+        both = [targets[: n_dp * n_tp][span], targets[n_dp * n_tp :][span]]
+        target = jnp.where(me == r, jnp.concatenate(both, axis=1), target)
+    solved_out[...] = solve(gram, target)
     for index, copy in enumerate(relays):
         copy.wait_send()
         if index not in (0, 1, 3, 5):
             copy.wait_recv()
     root_write = pltpu.make_async_copy(root, root_out, out_sem.at[0])
     root_write.start()
-    for copy in gram_copies:
-        copy.wait()
-    gram_out[...] = gram[...]
     root_write.wait()
 
 
-def solve_kernel(root_hbm, gram_ref, rhs_ref, grads_ref, root_out, pre_out, root, sems):
-    read = pltpu.make_async_copy(root_hbm, root, sems.at[0])
-    read.start()
-    system = gram_ref[...]
-    rows = system.shape[0]
-    eye = lax.broadcasted_iota(jnp.int32, system.shape, 0) == lax.broadcasted_iota(
-        jnp.int32, system.shape, 1
-    )
-    trace = jnp.sum(
-        jnp.sum(jnp.where(eye, system, 0.0), axis=0, keepdims=True), axis=1, keepdims=True
-    )
-    unit = 1.0 / (trace / rows)
-    system = system * unit + jnp.where(eye, 1.0, 0.0)
-    system_halves = halves(system)
-    first, steps = newton_plan(rows)
-    inverse = jnp.where(eye, 2.0 * first * steps[0], 0.0) - (first * first * steps[0]) * system
-    for scale in steps[1:]:
-        inverse_halves = halves(inverse)
-        residual = jnp.where(eye, 2.0, 0.0) - dot_halves(system_halves, inverse_halves)
-        inverse = scale * dot_halves(inverse_halves, halves(residual))
-    read.wait()
-    write = pltpu.make_async_copy(root, root_out, sems.at[1])
+def last_kernel(root_ref, solved_ref, grads_ref, root_out, pre_out, sem):
+    write = pltpu.make_async_copy(root_ref, root_out, sem.at[0])
     write.start()
-    target = rhs_ref[...] * unit
-    inverse_halves = halves(inverse)
-    solved = dot_halves(halves(target), inverse_halves)
-    for _ in range(2):
-        solved = solved + dot_halves(halves(target - dot_high(solved, system)), inverse_halves)
-    pre_out[...] = grads_ref[...] - dot_mid(solved, root[...])
+    pre_out[...] = grads_ref[...] - dot_mid(solved_ref[...], root_ref[...])
     write.wait()
 
 
@@ -506,27 +573,30 @@
     slots = activations.shape[0] // SEQ
     f32, bf16 = jnp.float32, jnp.bfloat16
     width, hidden = activations.shape[1], out_grads.shape[1]
-    phases = 5
-    hbm = pl.BlockSpec(memory_space=pl.ANY)
+    hbm = pl.BlockSpec(memory_space=pltpu.HBM)
+    anywhere = pl.BlockSpec(memory_space=pl.ANY)
     vmem = pl.BlockSpec(memory_space=pltpu.VMEM)
     smem = pl.BlockSpec(memory_space=pltpu.SMEM)
-    part_rows = -(-(rows // n_dp + slots) // 8) * 8
-    root, gram, rhs, grads = pl.pallas_call(
+    devices = n_dp * n_tp
+    part_rows = (3 * LANES + 2 * n_dp * slots) // n_dp
+    pin = functools.partial(pltpu.with_memory_space_constraint, memory_space=pltpu.HBM)
+    root, solved, grads = pl.pallas_call(
         functools.partial(fused_kernel, n_dp, n_tp),
         out_shape=(
             jax.ShapeDtypeStruct((rows, columns), f32),
-            jax.ShapeDtypeStruct((rows, rows), f32),
             jax.ShapeDtypeStruct((slots, rows), f32),
             jax.ShapeDtypeStruct((slots, columns), f32),
         ),
-        in_specs=[hbm, hbm, hbm, hbm, smem, smem, hbm, vmem, vmem],
-        out_specs=(hbm, vmem, vmem, vmem),
+        in_specs=[hbm, hbm, hbm, hbm, smem, smem, hbm, hbm, hbm],
+        out_specs=(anywhere, vmem, vmem),
         scratch_shapes=[
             pltpu.VMEM((slots, SEQ, width), bf16),
             pltpu.VMEM((slots, SEQ, hidden), bf16),
             pltpu.VMEM((RANK, width), bf16),
             pltpu.VMEM((RANK, hidden), bf16),
             pltpu.VMEM((rows, columns), f32),
+            pltpu.VMEM((slots, rows), f32),
+            pltpu.VMEM((rows, 2 * rows), f32),
             pltpu.VMEM((n_dp // 2, rows, LANES), f32),
             pltpu.VMEM((n_dp // 2, rows, LANES), f32),
             pltpu.VMEM((n_dp // 2, rows, LANES), f32),
@@ -534,50 +604,52 @@
             pltpu.VMEM((n_tp, SEQ, LANES), f32),
             pltpu.VMEM((RANK, LANES), f32),
             pltpu.VMEM((n_tp, n_dp, LANES), f32),
-            pltpu.VMEM((n_dp, n_tp, LANES), f32),
-            pltpu.VMEM((n_dp, n_tp, LANES), f32),
-            pltpu.VMEM((n_tp, 8, LANES), f32),
-            pltpu.VMEM((n_dp, 8, LANES), f32),
+            pltpu.VMEM((devices, 1, LANES), f32),
+            pltpu.VMEM((devices, 1, LANES), f32),
+            pltpu.VMEM((devices, 1, LANES), f32),
             pltpu.VMEM((rows, columns), f32),
-            pltpu.VMEM((n_dp, part_rows, rows), f32),
-            pltpu.VMEM((n_dp, part_rows, rows), f32),
-            pltpu.VMEM((n_tp, part_rows, rows), f32),
-            pltpu.VMEM((rows, rows), f32),
-            pltpu.SemaphoreType.DMA((3 + 2 * n_tp,)),
+            pltpu.VMEM((n_dp, part_rows, LANES), f32),
+            pltpu.VMEM((n_dp, part_rows, LANES), f32),
+            pltpu.VMEM((n_tp, part_rows, LANES), f32),
+            pltpu.VMEM((n_dp, part_rows, LANES), f32),
+            pltpu.SemaphoreType.DMA((5 + 2 * n_tp,)),
             pltpu.SemaphoreType.DMA((2, n_dp // 2)),
             pltpu.SemaphoreType.DMA((2, 3)),
             pltpu.SemaphoreType.DMA((2, 8)),
-            pltpu.SemaphoreType.DMA((phases, n_tp)),
-            pltpu.SemaphoreType.DMA((phases, n_tp)),
-            pltpu.SemaphoreType.DMA((phases, n_dp)),
-            pltpu.SemaphoreType.DMA((phases, n_dp)),
+            pltpu.SemaphoreType.DMA((3, n_tp)),
+            pltpu.SemaphoreType.DMA((3, n_tp)),
+            pltpu.SemaphoreType.DMA((2, n_dp)),
+            pltpu.SemaphoreType.DMA((2, n_dp)),
+            pltpu.SemaphoreType.DMA((2, devices)),
+            pltpu.SemaphoreType.DMA((2, devices)),
             pltpu.SemaphoreType.DMA((1,)),
+            pltpu.SemaphoreType.REGULAR,
         ],
         compiler_params=pltpu.CompilerParams(
-            collective_id=0, has_side_effects=True, vmem_limit_bytes=56 * 2**20
+            collective_id=0, has_side_effects=True, vmem_limit_bytes=32 * 2**20
         ),
     )(
-        activations,
-        out_grads,
-        input_proj.T,
-        grad_proj.T,
+        pin(activations),
+        pin(out_grads),
+        pin(input_proj.T),
+        pin(grad_proj.T),
         example_count,
         child_order,
-        prior_sketch,
-        fold_map.T,
-        merge_mix,
+        pin(prior_sketch),
+        pin(fold_map.T),
+        pin(merge_mix),
     )
     return pl.pallas_call(
-        solve_kernel,
+        last_kernel,
         out_shape=(
             jax.ShapeDtypeStruct((rows, columns), f32),
             jax.ShapeDtypeStruct((slots, columns), f32),
         ),
-        in_specs=[hbm, vmem, vmem, vmem],
-        out_specs=(hbm, vmem),
-        scratch_shapes=[pltpu.VMEM((rows, columns), f32), pltpu.SemaphoreType.DMA((2,))],
-        compiler_params=pltpu.CompilerParams(vmem_limit_bytes=56 * 2**20),
-    )(root, gram, rhs, grads)
+        in_specs=[vmem] * 3,
+        out_specs=(anywhere, vmem),
+        scratch_shapes=[pltpu.SemaphoreType.DMA((1,))],
+        compiler_params=pltpu.CompilerParams(vmem_limit_bytes=16 * 2**20),
+    )(root, solved, grads)
 
 
 def from_partner(value, axis, stride):
@@ -654,7 +726,8 @@
         and slots == n_tp
         and 2 * RANK == LANES
         and n_dp == 8
-        and rows % (8 * n_dp) == 0
+        and rows == 2 * LANES
+        and (3 * LANES + 2 * n_dp * slots) % (8 * n_dp) == 0
     )
 
 

time: 54.7 us -> 47.8 us (0.87)
  Pallas kernels: 53.2 us -> 45.7 us
  local copies, waits for them, and re-layouts: 0 us -> 0.65 us
    pallas_call x1, Pallas kernels: 6.51 us -> 1.63 us  [fused_body(): pl.pallas_call(last_kernel, out_shape=(jax.ShapeDtypeStruct((rows, column...]
    pallas_call x1, Pallas kernels: 46.7 us -> 44.1 us  [fused_body(): pl.pallas_call(functools.partial(fused_kernel, n_dp, n_tp), out_shape=(ja...]
    unnamed x0 -> x2, local copies, waits for them, and re-layouts: none -> 0.65 us
where the time goes in v1:
time: 47.8 us; the launch traced here: 47.7 us
  Pallas kernels  45.7 us (96%)
  between operations  1.29 us (3%)
  local copies, waits for them, and re-layouts  0.65 us (1%)
    pallas_call x1, Pallas kernels, fused_body(): pl.pallas_call(functools.partial(fused_kernel, n_dp, n_tp), out_shape=(ja...  44.1 us
    pallas_call x1, Pallas kernels, fused_body(): pl.pallas_call(last_kernel, out_shape=(jax.ShapeDtypeStruct((rows, column...  1.63 us

profile of v1, /device:TPU:0, one launch (start us, length us, event | category | flops | bytes accessed | tf_op | source)
XLA Modules:
  0.0 47.7 jit_solution(8278484171646134825)
XLA Ops:
  1.3 0.0 copy-start
  1.3 0.6 %copy-done = s32[8]{0:T(128)S(1)} copy-done((s32[8]{0:T(128)S(1)}, s32[8]{0:T(128)}, u32[]{:S(2)}) %copy-start) | copy-done | bytes 56
  1.9 44.1 %shard_map.104 = (f32[256,1024]{1,0:T(8,128)S(1)}, f32[4,256]{1,0:T(4,128)S(1)}, f32[4,1024]{1,0:T(4,128)S(1)}) custom-call(bf16[512,2048]{1,0:T(8,128)(2,1)} %act_hbm.1, bf16[512,7168]{1,0:T(8,128)(2,1)} %out_hbm.1, bf16[64,2048]{1,0:T(8,128)(2,1)} %bitcast.4, bf16[64,7168]{1,0:T(8,128)(2,1)} %bitcast.3, s32[1]{0:T(128)S(6)} %copy.11.count_ref, ...), custom_call_target="tpu_custom_call" | custom-call | tf_op jit(solution)/shard_map/pallas_call | solution.py:583
  46.0 1.6 %shard_map.105 = (f32[256,1024]{1,0:T(8,128)}, f32[4,1024]{1,0:T(4,128)}) custom-call(f32[256,1024]{1,0:T(8,128)S(1)} %get-tuple-element.5.root_ref, f32[4,256]{1,0:T(4,128)S(1)} %get-tuple-element.6.solved_ref, f32[4,1024]{1,0:T(4,128)S(1)} %get-tuple-element.7.grads_ref), custom_call_target="tpu_custom_call" | custom-call | tf_op jit(solution)/shard_map/pallas_call | solution.py:642
Async XLA Ops:
  1.3 0.7 %copy-start = (s32[8]{0:T(128)S(1)}, s32[8]{0:T(128)}, u32[]{:S(2)}) copy-start(s32[8]{0:T(128)} %order_ref.1) | copy-start | bytes 100

commit v2 on v1

--- a/solution.py
+++ b/solution.py
@@ -119,17 +119,17 @@
     wi_hbm,
     wo_hbm,
     count_ref,
-    order_ref,
+    order_hbm,
     prior_hbm,
     fold_hbm,
     mix_hbm,
     root_out,
-    solved_out,
+    gram_out,
+    target_out,
     grads_out,
-    act,
-    outg,
-    wi,
-    wo,
+    tokens,
+    weights,
+    order_ref,
     prior,
     fold_ref,
     mix_ref,
@@ -137,8 +137,10 @@
     node_send,
     node_recv,
     zsend,
+    zmid,
     zrecv,
     full,
+    slices_send,
     grads,
     grads_rows,
     grads_all,
@@ -149,15 +151,8 @@
     gram_z,
     gram_all,
     load_sem,
-    pair_sems,
-    node_sems,
+    sems,
     root_sems,
-    z_send,
-    z_recv,
-    p_send,
-    p_recv,
-    a_send,
-    a_recv,
     out_sem,
     ready_sem,
 ):
@@ -173,25 +168,34 @@
     def tp_of(k):
         return lax.rem(z + k, n_tp)
 
-    order = sorted(range(1, n_tp), key=lambda k: -min(k, n_tp - k)) + [0]
-    loads = []
-
-    def load(source, target):
-        copy = pltpu.make_async_copy(source, target, load_sem.at[len(loads)])
-        copy.start()
-        loads.append(copy)
-        return copy
+    width = act_hbm.shape[1]
+    near = z + 1 - 2 * lax.rem(z, 2)
+    far = z + 2 - 4 * (z // 2)
+    diagonal = near + 2 - 4 * (near // 2)
+    order = (diagonal, far, near, z)
+    used = []
+
+    def load(*pairs):
+        for source, target in pairs:
+            pltpu.make_async_copy(source, target, load_sem.at[len(used)]).start()
+        used.append(None)
+        return len(used) - 1
+
+    def drain(ref, sem):
+        pltpu.make_async_copy(ref, ref, sem).wait()
 
     def load_chunk(index):
-        span = pl.ds(pl.multiple_of(tp_of(order[index]) * SEQ, SEQ), SEQ)
-        return load(act_hbm.at[span], act.at[index]), load(out_hbm.at[span], outg.at[index])
-
-    weight_loads = [load(wi_hbm, wi), load(wo_hbm, wo)]
+        span = pl.ds(pl.multiple_of(order[index] * SEQ, SEQ), SEQ)
+        into = tokens.at[index]
+        return load((act_hbm.at[span], into.at[:, :width]), (out_hbm.at[span], into.at[:, width:]))
+
+    order_load = load((order_hbm, order_ref))
+    weight_load = load((wi_hbm, weights.at[:, :width]), (wo_hbm, weights.at[:, width:]))
     chunk_loads = [load_chunk(0)]
-    own_prior = load(prior_hbm, prior)
-    mix_load = load(mix_hbm, mix_ref)
+    prior_load = load((prior_hbm, prior))
+    mix_load = load((mix_hbm, mix_ref))
     chunk_loads += [load_chunk(index) for index in range(1, n_tp)]
-    fold_load = load(fold_hbm, fold_ref)
+    fold_load = load((fold_hbm, fold_ref))
 
     def tile_of(owner):
         return pl.ds(pl.multiple_of(owner * LANES, LANES), LANES)
@@ -212,95 +216,53 @@
     chip_y = chip + 2 - 4 * (chip // 2)
     chip_d = half - 1 - chip
 
-    def push(source, target, device, sems, index):
-        copy = pltpu.make_async_remote_copy(
+    PAIR, NODE, MID, SIDE, SLICE, ROW, SUM, SCATTER, ALONG, GATHER = range(10)
+
+    def push(phase, source, target, **device):
+        pltpu.make_async_remote_copy(
             src_ref=source,
             dst_ref=target,
-            send_sem=sems.at[0, index],
-            recv_sem=sems.at[1, index],
-            device_id={"dp": device},
+            send_sem=sems.at[0, phase],
+            recv_sem=sems.at[1, phase],
+            device_id=device,
             device_id_type=MESH,
-        )
-        copy.start()
-        return copy
-
-    pair_copies = [
-        push(prior_hbm.at[:, tile_of(2 * q + 1 - core)], pair_in.at[q], partner, pair_sems, q)
-        for q in range(half)
-    ]
+        ).start()
+
+    def received(phase, ref):
+        drain(ref, sems.at[1, phase])
+
+    for q in range(half):
+        push(PAIR, prior_hbm.at[:, tile_of(2 * q + 1 - core)], pair_in.at[q], dp=partner)
 
     def exchange(axis, phase, source, target):
         size, other = (n_tp, tp_of) if axis == "tensor" else (n_dp, dp_of)
-        send, recv = (z_send, z_recv) if axis == "tensor" else (p_send, p_recv)
-        copies = []
         for k in range(1, size):
-            copies.append(
-                pltpu.make_async_remote_copy(
-                    src_ref=source(other(k)),
-                    dst_ref=target,
-                    send_sem=send.at[phase, k],
-                    recv_sem=recv.at[phase, k],
-                    device_id={axis: other(k)},
-                    device_id_type=MESH,
-                )
-            )
-            copies[-1].start()
-        return copies
+            push(phase, source(other(k)), target, **{axis: other(k)})
 
     def exchange_all(phase, source, target):
-        copies = []
         for j in sorted(range(n_tp), key=lambda j: -min(j, n_tp - j)):
             for k in range(n_dp):
-                if j == 0 and k == 0:
-                    continue
-                copies.append(
-                    pltpu.make_async_remote_copy(
-                        src_ref=source(dp_of(k), tp_of(j)),
-                        dst_ref=target,
-                        send_sem=a_send.at[phase, j * n_dp + k],
-                        recv_sem=a_recv.at[phase, j * n_dp + k],
-                        device_id={"dp": dp_of(k), "tensor": tp_of(j)},
-                        device_id_type=MESH,
-                    )
-                )
-                copies[-1].start()
-        return copies
-
-    side_copies = []
-
-    def do_chunk(index):
-        k = order[index]
-        for copy in chunk_loads[index]:
-            copy.wait()
+                if (j, k) != (0, 0):
+                    push(phase, source(dp_of(k), tp_of(j)), target, dp=dp_of(k), tensor=tp_of(j))
+
+    def sides_of_chunk(index):
+        drain(tokens.at[index], load_sem.at[chunk_loads[index]])
         mid = SEQ // 2
-        right = [dot_flip(outg[index, h * mid : (h + 1) * mid], wo[...]) for h in range(2)]
-        left = [dot_flip(act[index, h * mid : (h + 1) * mid], wi[...]) for h in range(2)]
-        both = jnp.concatenate([jnp.concatenate(pair, axis=1) for pair in zip(left, right)], axis=0)
-        if k == 0:
-            zrecv[z] = both
-            return
-        zsend[index] = both
-        copy = pltpu.make_async_remote_copy(
-            src_ref=zsend.at[index],
-            dst_ref=zrecv.at[z],
-            send_sem=z_send.at[0, k],
-            recv_sem=z_recv.at[0, k],
-            device_id={"tensor": tp_of(k)},
-            device_id_type=MESH,
-        )
-        copy.start()
-        side_copies.append(copy)
-
-    for copy in weight_loads:
-        copy.wait()
-    do_chunk(0)
-
-    own_prior.wait()
-    mix_load.wait()
-    for copy in pair_copies:
-        copy.wait()
+        spans = [slice(h * mid, (h + 1) * mid) for h in range(2)]
+        right = [dot_flip(tokens[index, span, width:], weights[:, width:]) for span in spans]
+        left = [dot_flip(tokens[index, span, :width], weights[:, :width]) for span in spans]
+        return jnp.concatenate([jnp.concatenate(pair, axis=1) for pair in zip(left, right)], axis=0)
+
+    drain(weights, load_sem.at[weight_load])
+    zsend[0] = sides_of_chunk(0)
+    push(MID, zsend.at[0], zmid, tensor=near)
+
+    drain(order_ref, load_sem.at[order_load])
+    drain(prior, load_sem.at[prior_load])
+    drain(mix_ref, load_sem.at[mix_load])
+    received(PAIR, pair_in)
     first_mix, second_mix = mix_ref[:, :rows], mix_ref[:, rows:]
-    own_first = order_ref[2 * chip] == core
+    own_first = order_ref[0, 2 * chip] == core
     own_half = [prior[:, tile_of(2 * q + core)] for q in range(half)]
     firsts = [jnp.where(own_first, own_half[q], pair_in[q]) for q in range(half)]
     seconds = [jnp.where(own_first, pair_in[q], own_half[q]) for q in range(half)]
@@ -309,15 +271,18 @@
     mixed = mixed + dot_halves(second_halves, halves(jnp.concatenate(seconds, axis=1)))
     for q in range(half):
         node_send[q] = mixed[:, q * LANES : (q + 1) * LANES]
-    node_copies = [
-        push(node_send.at[other], node_recv.at[chip], 2 * other + core, node_sems, index)
-        for index, other in enumerate((chip_x, chip_y, chip_d))
-    ]
+    for other in (chip_x, chip_y, chip_d):
+        push(NODE, node_send.at[other], node_recv.at[chip], dp=2 * other + core)
     node_recv[chip] = node_send[chip]
-    for index in range(1, n_tp):
-        do_chunk(index)
-
-    fold_load.wait()
+    far_sides = sides_of_chunk(1)
+    zsend[2] = sides_of_chunk(2)
+    received(MID, zmid)
+    zsend[1] = far_sides + zmid[...]
+    push(SIDE, zsend.at[1], zrecv.at[1], tensor=far)
+    push(SIDE, zsend.at[2], zrecv.at[0], tensor=near)
+    own_sides = sides_of_chunk(3)
+
+    drain(fold_ref, load_sem.at[fold_load])
     fold_rows = fold_ref[...]
     paths = [[jnp.concatenate([dot_rows(fold_rows, first_mix), dot_rows(fold_rows, second_mix)], axis=0)]]
     for level in range(1, levels):
@@ -327,11 +292,8 @@
     paths = [[stacked(p, (0, 0, 1)).T.astype(jnp.bfloat16) for p in level] for level in paths]
     fold = fold_rows.T
 
-    for copy in side_copies:
-        copy.wait()
-    sides = zrecv[0]
-    for index in range(1, n_tp):
-        sides = sides + zrecv[index]
+    received(SIDE, zrecv)
+    sides = (own_sides + zrecv[0]) + zrecv[1]
     lane = lax.broadcasted_iota(jnp.int32, sides.shape, 1)
     doubled = jnp.where(lane < RANK, sides, pltpu.roll(sides, RANK, 1))
     product = dot_mid(sides.T, doubled) / jnp.sqrt(f32(SEQ))
@@ -344,16 +306,16 @@
     for row in range(n_tp * n_dp):
         grads_rows[row] = mine[row : row + 1]
     for index in range(n_tp):
-        zsend[n_tp + index, 0:n_dp, :] = mine[index * n_dp : (index + 1) * n_dp]
-    grads[z] = zsend[n_tp + z, 0:n_dp, :]
+        slices_send[index] = mine[index * n_dp : (index + 1) * n_dp]
+    grads[z] = slices_send[z]
     slot = me * n_tp + z
     grads_all[slot] = grads_rows[z * n_dp + me]
     pl.semaphore_wait(ready_sem, n_dp - 1)
-    grad_copies = exchange("tensor", 1, lambda t: zsend.at[n_tp + t, 0:n_dp, :], grads.at[z])
-    row_copies = exchange_all(0, lambda d, t: grads_rows.at[t * n_dp + d], grads_all.at[slot])
+    exchange("tensor", SLICE, lambda t: slices_send.at[t], grads.at[z])
+    exchange_all(ROW, lambda d, t: grads_rows.at[t * n_dp + d], grads_all.at[slot])
 
     flags = [
-        [order_ref[j * 2 ** (level + 1) + 2**level - 1] == 1 for j in range(n_dp >> (level + 1))]
+        [order_ref[0, j * 2 ** (level + 1) + 2**level - 1] == 1 for j in range(n_dp >> (level + 1))]
         for level in range(levels)
     ]
 
@@ -364,8 +326,7 @@
     def total(value):
         return jnp.sum(jnp.sum(value, axis=0, keepdims=True), axis=1, keepdims=True)
 
-    for copy in node_copies:
-        copy.wait()
+    received(NODE, node_recv.at[: half - 1])
     mixtures = [[[node_recv[j]] for j in range(half)]]
     for level in range(1, levels):
         below = mixtures[-1]
@@ -384,8 +345,7 @@
             ]
         )
 
-    for copy in grad_copies:
-        copy.wait()
+    received(SLICE, grads.at[: n_tp - 1])
     leaf_square = jnp.zeros((rows, LANES), f32)
     for tile in range(n_dp):
         leaf = prior[:, tile * LANES : (tile + 1) * LANES]
@@ -396,8 +356,7 @@
         leaf_square = leaf_square + leaf * leaf
     own_mass = total(leaf_square)
 
-    for copy in row_copies:
-        copy.wait()
+    received(ROW, grads_all.at[: n_tp * n_dp - 1])
     steps_of = [
         [jnp.concatenate([grads_all[r * n_tp + e] for e in range(n_tp)], axis=0)] for r in range(n_dp)
     ]
@@ -440,8 +399,8 @@
     for index, value in enumerate(sums):
         packed = jnp.where(lane == n_dp + index, value, packed)
     sums_all[slot] = packed
-    for copy in exchange_all(1, lambda d, t: sums_all.at[slot], sums_all.at[slot]):
-        copy.wait()
+    exchange_all(SUM, lambda d, t: sums_all.at[slot], sums_all.at[slot])
+    received(SUM, sums_all.at[: n_tp * n_dp - 1])
     parts_of = [sums_all[index] for index in range(n_tp * n_dp)]
     while len(parts_of) > 1:
         parts_of = [a + b for a, b in zip(parts_of[0::2], parts_of[1::2])]
@@ -491,70 +450,96 @@
     for r in range(n_dp):
         gram_part[r] = triangle[r * part_rows : (r + 1) * part_rows]
     gram_rs[me] = gram_part[me]
-    gram_copies = exchange("dp", 0, lambda t: gram_part.at[t], gram_rs.at[me])
+    exchange("dp", SCATTER, lambda t: gram_part.at[t], gram_rs.at[me])
     dev_x, dev_y, dev_d = (2 * other + core for other in (chip_x, chip_y, chip_d))
     upper, lower = pl.ds(0, rows // 2), pl.ds(rows // 2, rows // 2)
 
     def relay(index, owner, device, span=slice(None)):
         block_of = root.at[span, tile_of(owner)]
-        return push(block_of, block_of, device, root_sems, index)
-
-    relays = [relay(0, me, dev_x), relay(1, me, dev_y), relay(2, me, partner)]
-    for copy in gram_copies:
-        copy.wait()
+        pltpu.make_async_remote_copy(
+            src_ref=block_of,
+            dst_ref=block_of,
+            send_sem=root_sems.at[5],
+            recv_sem=root_sems.at[index],
+            device_id={"dp": device},
+            device_id_type=MESH,
+        ).start()
+
+    def relayed(index, count):
+        drain(root.at[:, : count * LANES] if count else root.at[upper, :LANES], root_sems.at[index])
+
+    relay(0, me, dev_x)
+    relay(1, me, dev_y)
+    relay(4, me, partner)
+    received(SCATTER, gram_rs.at[: n_dp - 1])
     part = gram_rs[0]
     for index in range(1, n_dp):
         part = part + gram_rs[index]
     gram_z[z] = part
-    z_copies = exchange("tensor", 2, lambda t: gram_z.at[z], gram_z.at[z])
-    relays[0].wait_recv()
-    relays.append(relay(3, dev_x, dev_y, upper))
-    relays.append(relay(4, dev_x, partner))
-    relays[1].wait_recv()
-    relays.append(relay(5, dev_y, dev_x, lower))
-    relays.append(relay(6, dev_y, partner))
-    for copy in z_copies:
-        copy.wait()
+    exchange("tensor", ALONG, lambda t: gram_z.at[z], gram_z.at[z])
+    relayed(0, 1)
+    relay(2, dev_x, dev_y, upper)
+    relay(4, dev_x, partner)
+    relayed(1, 1)
+    relay(3, dev_y, dev_x, lower)
+    relay(4, dev_y, partner)
+    received(ALONG, gram_z.at[: n_tp - 1])
     part = gram_z[0]
     for index in range(1, n_tp):
         part = part + gram_z[index]
     gram_all[me] = part
-    gram_copies = exchange("dp", 1, lambda t: gram_all.at[me], gram_all.at[me])
-    relays[3].wait_recv()
-    relays[5].wait_recv()
-    relays.append(relay(7, dev_d, partner))
-    for copy in gram_copies:
-        copy.wait()
+    exchange("dp", GATHER, lambda t: gram_all.at[me], gram_all.at[me])
+    relayed(2, 0)
+    relayed(3, 0)
+    relay(4, dev_d, partner)
+    relayed(4, half)
+    root_write = pltpu.make_async_copy(root, root_out, out_sem.at[0])
+    root_write.start()
+    for phase, ref in (
+        (PAIR, pair_in),
+        (NODE, node_recv.at[: half - 1]),
+        (MID, zmid),
+        (SIDE, zrecv),
+        (SLICE, grads.at[: n_tp - 1]),
+        (ROW, grads_all.at[: n_tp * n_dp - 1]),
+        (SUM, sums_all.at[: n_tp * n_dp - 1]),
+        (SCATTER, gram_rs.at[: n_dp - 1]),
+        (ALONG, gram_z.at[: n_tp - 1]),
+    ):
+        drain(ref, sems.at[0, phase])
+    received(GATHER, gram_all.at[: n_dp - 1])
     triangle = jnp.concatenate([gram_all[r] for r in range(n_dp)], axis=0)
-    corner = triangle[LANES:rows]
-    gram = jnp.concatenate(
-        [
-            jnp.concatenate([triangle[:LANES], corner.T], axis=1),
-            jnp.concatenate([corner, triangle[rows : rows + LANES]], axis=1),
-        ],
-        axis=0,
-    )
+    gram_out[...] = triangle[: rows + LANES]
     targets = triangle[rows + LANES :]
     target = jnp.zeros((n_tp, rows), f32)
     for r in range(n_dp):
         span = slice(r * n_tp, (r + 1) * n_tp)
         both = [targets[: n_dp * n_tp][span], targets[n_dp * n_tp :][span]]
         target = jnp.where(me == r, jnp.concatenate(both, axis=1), target)
-    solved_out[...] = solve(gram, target)
-    for index, copy in enumerate(relays):
-        copy.wait_send()
-        if index not in (0, 1, 3, 5):
-            copy.wait_recv()
-    root_write = pltpu.make_async_copy(root, root_out, out_sem.at[0])
-    root_write.start()
+    target_out[...] = target
+    drain(gram_all.at[: n_dp - 1], sems.at[0, GATHER])
+    drain(root.at[:, : (n_dp - 1) * LANES], root_sems.at[5])
     root_write.wait()
 
 
-def last_kernel(root_ref, solved_ref, grads_ref, root_out, pre_out, sem):
+def last_kernel(root_ref, gram_ref, target_ref, grads_ref, root_out, pre_out, pre, sem):
     write = pltpu.make_async_copy(root_ref, root_out, sem.at[0])
     write.start()
-    pre_out[...] = grads_ref[...] - dot_mid(solved_ref[...], root_ref[...])
+    rows = root_ref.shape[0]
+    corner = gram_ref[LANES:rows]
+    gram = jnp.concatenate(
+        [
+            jnp.concatenate([gram_ref[:LANES], corner.T], axis=1),
+            jnp.concatenate([corner, gram_ref[rows:]], axis=1),
+        ],
+        axis=0,
+    )
+    solved = solve(gram, target_ref[...])
+    pre[...] = grads_ref[...] - dot_mid(solved, root_ref[...])
+    pre_write = pltpu.make_async_copy(pre, pre_out, sem.at[1])
+    pre_write.start()
     write.wait()
+    pre_write.wait()
 
 
 def fused_body(
@@ -580,29 +565,31 @@
     devices = n_dp * n_tp
     part_rows = (3 * LANES + 2 * n_dp * slots) // n_dp
     pin = functools.partial(pltpu.with_memory_space_constraint, memory_space=pltpu.HBM)
-    root, solved, grads = pl.pallas_call(
+    root, gram, target, grads = pl.pallas_call(
         functools.partial(fused_kernel, n_dp, n_tp),
         out_shape=(
             jax.ShapeDtypeStruct((rows, columns), f32),
+            jax.ShapeDtypeStruct((3 * LANES, LANES), f32),
             jax.ShapeDtypeStruct((slots, rows), f32),
             jax.ShapeDtypeStruct((slots, columns), f32),
         ),
-        in_specs=[hbm, hbm, hbm, hbm, smem, smem, hbm, hbm, hbm],
-        out_specs=(anywhere, vmem, vmem),
+        in_specs=[hbm, hbm, hbm, hbm, smem, hbm, hbm, hbm, hbm],
+        out_specs=(anywhere, vmem, vmem, vmem),
         scratch_shapes=[
-            pltpu.VMEM((slots, SEQ, width), bf16),
-            pltpu.VMEM((slots, SEQ, hidden), bf16),
-            pltpu.VMEM((RANK, width), bf16),
-            pltpu.VMEM((RANK, hidden), bf16),
+            pltpu.VMEM((slots, SEQ, width + hidden), bf16),
+            pltpu.VMEM((RANK, width + hidden), bf16),
+            pltpu.SMEM((1, n_dp), jnp.int32),
             pltpu.VMEM((rows, columns), f32),
             pltpu.VMEM((slots, rows), f32),
             pltpu.VMEM((rows, 2 * rows), f32),
             pltpu.VMEM((n_dp // 2, rows, LANES), f32),
             pltpu.VMEM((n_dp // 2, rows, LANES), f32),
             pltpu.VMEM((n_dp // 2, rows, LANES), f32),
-            pltpu.VMEM((2 * n_tp, SEQ, LANES), f32),
-            pltpu.VMEM((n_tp, SEQ, LANES), f32),
+            pltpu.VMEM((3, SEQ, LANES), f32),
+            pltpu.VMEM((SEQ, LANES), f32),
+            pltpu.VMEM((2, SEQ, LANES), f32),
             pltpu.VMEM((RANK, LANES), f32),
+            pltpu.VMEM((n_tp, n_dp, LANES), f32),
             pltpu.VMEM((n_tp, n_dp, LANES), f32),
             pltpu.VMEM((devices, 1, LANES), f32),
             pltpu.VMEM((devices, 1, LANES), f32),
@@ -612,16 +599,9 @@
             pltpu.VMEM((n_dp, part_rows, LANES), f32),
             pltpu.VMEM((n_tp, part_rows, LANES), f32),
             pltpu.VMEM((n_dp, part_rows, LANES), f32),
-            pltpu.SemaphoreType.DMA((5 + 2 * n_tp,)),
-            pltpu.SemaphoreType.DMA((2, n_dp // 2)),
-            pltpu.SemaphoreType.DMA((2, 3)),
-            pltpu.SemaphoreType.DMA((2, 8)),
-            pltpu.SemaphoreType.DMA((3, n_tp)),
-            pltpu.SemaphoreType.DMA((3, n_tp)),
-            pltpu.SemaphoreType.DMA((2, n_dp)),
-            pltpu.SemaphoreType.DMA((2, n_dp)),
-            pltpu.SemaphoreType.DMA((2, devices)),
-            pltpu.SemaphoreType.DMA((2, devices)),
+            pltpu.SemaphoreType.DMA((9,)),
+            pltpu.SemaphoreType.DMA((2, 10)),
+            pltpu.SemaphoreType.DMA((6,)),
             pltpu.SemaphoreType.DMA((1,)),
             pltpu.SemaphoreType.REGULAR,
         ],
@@ -634,7 +614,7 @@
         pin(input_proj.T),
         pin(grad_proj.T),
         example_count,
-        child_order,
+        pin(child_order.reshape(1, n_dp)),
         pin(prior_sketch),
         pin(fold_map.T),
         pin(merge_mix),
@@ -645,11 +625,11 @@
             jax.ShapeDtypeStruct((rows, columns), f32),
             jax.ShapeDtypeStruct((slots, columns), f32),
         ),
-        in_specs=[vmem] * 3,
-        out_specs=(anywhere, vmem),
-        scratch_shapes=[pltpu.SemaphoreType.DMA((1,))],
+        in_specs=[vmem] * 4,
+        out_specs=(anywhere, anywhere),
+        scratch_shapes=[pltpu.VMEM((slots, columns), f32), pltpu.SemaphoreType.DMA((2,))],
         compiler_params=pltpu.CompilerParams(vmem_limit_bytes=16 * 2**20),
-    )(root, solved, grads)
+    )(root, gram, target, grads)
 
 
 def from_partner(value, axis, stride):
@@ -726,6 +706,7 @@
         and slots == n_tp
         and 2 * RANK == LANES
         and n_dp == 8
+        and n_tp == 4
         and rows == 2 * LANES
         and (3 * LANES + 2 * n_dp * slots) % (8 * n_dp) == 0
     )

time: 47.8 us -> 44 us (0.921)
  Pallas kernels: 45.7 us -> 42.5 us
  local copies, waits for them, and re-layouts: 0.65 us -> 0 us
    pallas_call x1, Pallas kernels: 44.1 us -> 38.2 us  [fused_body(): pl.pallas_call(functools.partial(fused_kernel, n_dp, n_tp), out_shape=(ja...]
    pallas_call x1, Pallas kernels: 1.63 us -> 4.32 us  [fused_body(): pl.pallas_call(last_kernel, out_shape=(jax.ShapeDtypeStruct((rows, column...]
    unnamed x2 -> x0, local copies, waits for them, and re-layouts: 0.65 us -> none
where the time goes in v2:
time: 44 us; the launch traced here: 43.8 us
  Pallas kernels  42.5 us (97%)
  between operations  1.29 us (3%)
    pallas_call x1, Pallas kernels, fused_body(): pl.pallas_call(functools.partial(fused_kernel, n_dp, n_tp), out_shape=(ja...  38.2 us
    pallas_call x1, Pallas kernels, fused_body(): pl.pallas_call(last_kernel, out_shape=(jax.ShapeDtypeStruct((rows, column...  4.32 us

profile of v2, /device:TPU:0, one launch (start us, length us, event | category | flops | bytes accessed | tf_op | source)
XLA Modules:
  0.0 43.8 jit_solution(14054339741628528514)
XLA Ops:
  1.3 38.2 %shard_map.104 = (f32[256,1024]{1,0:T(8,128)S(1)}, f32[384,128]{1,0:T(8,128)S(1)}, f32[4,256]{1,0:T(4,128)S(1)}, f32[4,1024]{1,0:T(4,128)S(1)}) custom-call(bf16[512,2048]{1,0:T(8,128)(2,1)} %act_hbm.1, bf16[512,7168]{1,0:T(8,128)(2,1)} %out_hbm.1, bf16[64,2048]{1,0:T(8,128)(2,1)} %bitcast.5, bf16[64,7168]{1,0:T(8,128)(2,1)} %bitcast.4, ...), custom_call_target="tpu_custom_call" | custom-call | tf_op jit(solution)/shard_map/pallas_call | solution.py:568
  39.5 4.3 %shard_map.105 = (f32[256,1024]{1,0:T(8,128)}, f32[4,1024]{1,0:T(4,128)}) custom-call(f32[256,1024]{1,0:T(8,128)S(1)} %get-tuple-element.6.root_ref, f32[384,128]{1,0:T(8,128)S(1)} %get-tuple-element.7.gram_ref, f32[4,256]{1,0:T(4,128)S(1)} %get-tuple-element.8.target_ref, f32[4,1024]{1,0:T(4,128)S(1)} %get-tuple-element.9.grads_ref), custom_call_target="tpu_custom_call" | custom-call | tf_op jit(solution)/shard_map/pallas_call | solution.py:622

commit v3 on v2

--- a/solution.py
+++ b/solution.py
@@ -144,6 +144,9 @@
     grads,
     grads_rows,
     grads_all,
+    peer_all,
+    mix_send,
+    mix_recv,
     sums_all,
     root,
     gram_part,
@@ -172,7 +175,7 @@
     near = z + 1 - 2 * lax.rem(z, 2)
     far = z + 2 - 4 * (z // 2)
     diagonal = near + 2 - 4 * (near // 2)
-    order = (diagonal, far, near, z)
+    order = (diagonal, near, far, z)
     used = []
 
     def load(*pairs):
@@ -216,7 +219,7 @@
     chip_y = chip + 2 - 4 * (chip // 2)
     chip_d = half - 1 - chip
 
-    PAIR, NODE, MID, SIDE, SLICE, ROW, SUM, SCATTER, ALONG, GATHER = range(10)
+    PAIR, NODE, MID, SIDE, SLICE, ROW, PEER, SUM, SCATTER, ALONG, GATHER, MIX = range(12)
 
     def push(phase, source, target, **device):
         pltpu.make_async_remote_copy(
@@ -274,12 +277,12 @@
     for other in (chip_x, chip_y, chip_d):
         push(NODE, node_send.at[other], node_recv.at[chip], dp=2 * other + core)
     node_recv[chip] = node_send[chip]
-    far_sides = sides_of_chunk(1)
-    zsend[2] = sides_of_chunk(2)
+    zsend[1] = sides_of_chunk(1)
+    push(SIDE, zsend.at[1], zrecv.at[0], tensor=near)
+    far_sides = sides_of_chunk(2)
     received(MID, zmid)
-    zsend[1] = far_sides + zmid[...]
-    push(SIDE, zsend.at[1], zrecv.at[1], tensor=far)
-    push(SIDE, zsend.at[2], zrecv.at[0], tensor=near)
+    zsend[2] = far_sides + zmid[...]
+    push(SIDE, zsend.at[2], zrecv.at[1], tensor=far)
     own_sides = sides_of_chunk(3)
 
     drain(fold_ref, load_sem.at[fold_load])
@@ -345,6 +348,10 @@
             ]
         )
 
+    for index, part in enumerate(mixtures[-1][0]):
+        mix_send[index] = part
+    push(MIX, mix_send, mix_recv, dp=partner)
+
     received(SLICE, grads.at[: n_tp - 1])
     leaf_square = jnp.zeros((rows, LANES), f32)
     for tile in range(n_dp):
@@ -357,21 +364,26 @@
     own_mass = total(leaf_square)
 
     received(ROW, grads_all.at[: n_tp * n_dp - 1])
-    steps_of = [
-        [jnp.concatenate([grads_all[r * n_tp + e] for e in range(n_tp)], axis=0)] for r in range(n_dp)
-    ]
-    every = jnp.concatenate([step[0] for step in steps_of], axis=0)
-    every_halves = halves(every)
-    sums, products, nodes = [], [], []
-    for level in range(levels):
-        level_products, level_nodes, merged_steps = [], [], []
+    push(PEER, grads_all, peer_all, dp=partner)
+
+    def steps_from(rows_of):
+        steps_of = [
+            [jnp.concatenate([rows_of[r * n_tp + e] for e in range(n_tp)], axis=0)] for r in range(n_dp)
+        ]
+        return steps_of, jnp.concatenate([step[0] for step in steps_of], axis=0)
+
+    def merge_steps(level, steps_of):
+        merged_steps = []
         for j in range(len(steps_of) // 2):
             first, second = pick(flags[level][j], steps_of[2 * j], steps_of[2 * j + 1])
             if level == 0:
                 merged_steps.append([jnp.concatenate([first[0], second[0]], axis=0)])
             else:
                 merged_steps.append(first + second)
-        updates = [
+        return merged_steps
+
+    def updates_of(level, merged_steps):
+        return [
             jnp.dot(
                 path,
                 jnp.concatenate([stacked(g[i], (0, 1, 0)) for g in merged_steps], axis=1).astype(jnp.bfloat16),
@@ -379,6 +391,13 @@
             )
             for i, path in enumerate(paths[level])
         ]
+
+    steps_of, every = steps_from(grads_all)
+    sums, products, nodes = [], [], []
+    for level in range(levels):
+        level_products, level_nodes = [], []
+        merged_steps = merge_steps(level, steps_of)
+        updates = updates_of(level, merged_steps)
         for j in range(len(merged_steps)):
             parts = [
                 v + update[:, j * LANES : (j + 1) * LANES]
@@ -400,6 +419,13 @@
         packed = jnp.where(lane == n_dp + index, value, packed)
     sums_all[slot] = packed
     exchange_all(SUM, lambda d, t: sums_all.at[slot], sums_all.at[slot])
+    received(PEER, peer_all)
+    received(MIX, mix_recv)
+    steps_of, peer_every = steps_from(peer_all)
+    for level in range(levels):
+        steps_of = merge_steps(level, steps_of)
+    peer_parts = [mix_recv[i] + update for i, update in enumerate(updates_of(levels - 1, steps_of))]
+    every_halves = halves(jnp.concatenate([every, peer_every], axis=1))
     received(SUM, sums_all.at[: n_tp * n_dp - 1])
     parts_of = [sums_all[index] for index in range(n_tp * n_dp)]
     while len(parts_of) > 1:
@@ -430,12 +456,16 @@
             new_masses.append(mass)
             new_scales.append([scale * c for c in coefs])
         masses, scales = new_masses, new_scales
-    chunk = scales[0][0] * nodes[0][0]
-    for c, part in zip(scales[0][1:], nodes[0][1:]):
-        chunk = chunk + c * part
-    root[:, tile_of(me)] = chunk
-
-    chunk_halves = halves(chunk)
+    chunks = []
+    for parts in (nodes[0], peer_parts):
+        chunk = scales[0][0] * parts[0]
+        for c, part in zip(scales[0][1:], parts[1:]):
+            chunk = chunk + c * part
+        chunks.append(chunk)
+    root[:, tile_of(me)] = chunks[0]
+    root[:, tile_of(partner)] = chunks[1]
+
+    chunk_halves = halves(jnp.concatenate(chunks, axis=1))
     upper_halves, lower_halves = [[v[s] for v in chunk_halves] for s in (slice(0, LANES), slice(LANES, rows))]
     targets = dot_flip_halves(every_halves, chunk_halves)
     triangle = jnp.concatenate(
@@ -449,8 +479,9 @@
     )
     for r in range(n_dp):
         gram_part[r] = triangle[r * part_rows : (r + 1) * part_rows]
-    gram_rs[me] = gram_part[me]
-    exchange("dp", SCATTER, lambda t: gram_part.at[t], gram_rs.at[me])
+    gram_rs[chip] = gram_part[me]
+    for other in (chip_d, chip_x, chip_y):
+        push(SCATTER, gram_part.at[2 * other + core], gram_rs.at[chip], dp=2 * other + core)
     dev_x, dev_y, dev_d = (2 * other + core for other in (chip_x, chip_y, chip_d))
     upper, lower = pl.ds(0, rows // 2), pl.ds(rows // 2, rows // 2)
 
@@ -470,10 +501,9 @@
 
     relay(0, me, dev_x)
     relay(1, me, dev_y)
-    relay(4, me, partner)
-    received(SCATTER, gram_rs.at[: n_dp - 1])
+    received(SCATTER, gram_rs.at[: half - 1])
     part = gram_rs[0]
-    for index in range(1, n_dp):
+    for index in range(1, half):
         part = part + gram_rs[index]
     gram_z[z] = part
     exchange("tensor", ALONG, lambda t: gram_z.at[z], gram_z.at[z])
@@ -492,7 +522,7 @@
     relayed(2, 0)
     relayed(3, 0)
     relay(4, dev_d, partner)
-    relayed(4, half)
+    relayed(4, half - 1)
     root_write = pltpu.make_async_copy(root, root_out, out_sem.at[0])
     root_write.start()
     for phase, ref in (
@@ -503,7 +533,9 @@
         (SLICE, grads.at[: n_tp - 1]),
         (ROW, grads_all.at[: n_tp * n_dp - 1]),
         (SUM, sums_all.at[: n_tp * n_dp - 1]),
-        (SCATTER, gram_rs.at[: n_dp - 1]),
+        (PEER, peer_all),
+        (MIX, mix_recv),
+        (SCATTER, gram_rs.at[: half - 1]),
         (ALONG, gram_z.at[: n_tp - 1]),
     ):
         drain(ref, sems.at[0, phase])
@@ -518,7 +550,7 @@
         target = jnp.where(me == r, jnp.concatenate(both, axis=1), target)
     target_out[...] = target
     drain(gram_all.at[: n_dp - 1], sems.at[0, GATHER])
-    drain(root.at[:, : (n_dp - 1) * LANES], root_sems.at[5])
+    drain(root.at[:, : (n_dp - 2) * LANES], root_sems.at[5])
     root_write.wait()
 
 
@@ -594,13 +626,16 @@
             pltpu.VMEM((devices, 1, LANES), f32),
             pltpu.VMEM((devices, 1, LANES), f32),
             pltpu.VMEM((devices, 1, LANES), f32),
+            pltpu.VMEM((n_dp // 2, rows, LANES), f32),
+            pltpu.VMEM((n_dp // 2, rows, LANES), f32),
+            pltpu.VMEM((devices, 1, LANES), f32),
             pltpu.VMEM((rows, columns), f32),
             pltpu.VMEM((n_dp, part_rows, LANES), f32),
-            pltpu.VMEM((n_dp, part_rows, LANES), f32),
+            pltpu.VMEM((n_dp // 2, part_rows, LANES), f32),
             pltpu.VMEM((n_tp, part_rows, LANES), f32),
             pltpu.VMEM((n_dp, part_rows, LANES), f32),
             pltpu.SemaphoreType.DMA((9,)),
-            pltpu.SemaphoreType.DMA((2, 10)),
+            pltpu.SemaphoreType.DMA((2, 12)),
             pltpu.SemaphoreType.DMA((6,)),
             pltpu.SemaphoreType.DMA((1,)),
             pltpu.SemaphoreType.REGULAR,

time: 44 us -> 42.9 us (0.975)
  Pallas kernels: 42.5 us -> 41.5 us
    pallas_call x1, Pallas kernels: 38.2 us -> 37.2 us  [fused_body(): pl.pallas_call(functools.partial(fused_kernel, n_dp, n_tp), out_shape=(ja...]
where the time goes in v3:
time: 42.9 us; the launch traced here: 42.8 us
  Pallas kernels  41.5 us (97%)
  between operations  1.29 us (3%)
    pallas_call x1, Pallas kernels, fused_body(): pl.pallas_call(functools.partial(fused_kernel, n_dp, n_tp), out_shape=(ja...  37.2 us
    pallas_call x1, Pallas kernels, fused_body(): pl.pallas_call(last_kernel, out_shape=(jax.ShapeDtypeStruct((rows, column...  4.32 us

profile of v3, /device:TPU:0, one launch (start us, length us, event | category | flops | bytes accessed | tf_op | source)
XLA Modules:
  0.0 42.8 jit_solution(4070581033619294593)
XLA Ops:
  1.3 37.2 %shard_map.104 = (f32[256,1024]{1,0:T(8,128)S(1)}, f32[384,128]{1,0:T(8,128)S(1)}, f32[4,256]{1,0:T(4,128)S(1)}, f32[4,1024]{1,0:T(4,128)S(1)}) custom-call(bf16[512,2048]{1,0:T(8,128)(2,1)} %act_hbm.1, bf16[512,7168]{1,0:T(8,128)(2,1)} %out_hbm.1, bf16[64,2048]{1,0:T(8,128)(2,1)} %bitcast.5, bf16[64,7168]{1,0:T(8,128)(2,1)} %bitcast.4, ...), custom_call_target="tpu_custom_call" | custom-call | tf_op jit(solution)/shard_map/pallas_call | solution.py:600
  38.4 4.3 %shard_map.105 = (f32[256,1024]{1,0:T(8,128)}, f32[4,1024]{1,0:T(4,128)}) custom-call(f32[256,1024]{1,0:T(8,128)S(1)} %get-tuple-element.6.root_ref, f32[384,128]{1,0:T(8,128)S(1)} %get-tuple-element.7.gram_ref, f32[4,256]{1,0:T(4,128)S(1)} %get-tuple-element.8.target_ref, f32[4,1024]{1,0:T(4,128)S(1)} %get-tuple-element.9.grads_ref), custom_call_target="tpu_custom_call" | custom-call | tf_op jit(solution)/shard_map/pallas_call | solution.py:657

commit v4 on v3

--- a/solution.py
+++ b/solution.py
@@ -61,20 +61,33 @@
     return dot_flip(jnp.concatenate([a, a, b], axis=1), jnp.concatenate([c, d, c], axis=1))
 
 
-def dot_split(left, right):
+def dot_rows_halved(left, right):
     (a, b), (c, d) = left, right
-    half = a.shape[1] // 2
-    first = jnp.dot(
-        jnp.concatenate([a, b[:, :half]], axis=1),
-        jnp.concatenate([c, c[:half]], axis=0),
-        preferred_element_type=jnp.float32,
+    left = jnp.concatenate([a, a, b], axis=1)
+    right = jnp.concatenate([c, d, c], axis=0)
+    half = left.shape[0] // 2
+    return jnp.concatenate(
+        [
+            jnp.dot(left[:half], right, preferred_element_type=jnp.float32),
+            jnp.dot(left[half:], right, preferred_element_type=jnp.float32),
+        ],
+        axis=0,
     )
-    second = jnp.dot(
-        jnp.concatenate([a, b[:, half:]], axis=1),
-        jnp.concatenate([d, c[half:]], axis=0),
-        preferred_element_type=jnp.float32,
-    )
-    return first + second
+
+
+def thirds(value):
+    high, rest = halves(value)
+    rest = value - high.astype(jnp.float32)
+    return (high, *halves(rest))
+
+
+def dot_thirds(left, right):
+    count = left.shape[0]
+    stack = jnp.concatenate(thirds(left), axis=0)
+    a, b, c = (jnp.dot(stack, part, preferred_element_type=jnp.float32) for part in thirds(right))
+    high = a[count : 2 * count] + b[:count]
+    low = (a[2 * count :] + b[count : 2 * count]) + c[:count]
+    return a[:count] + (high + low)
 
 
 def stacked(value, order):
@@ -83,32 +96,27 @@
     return jnp.concatenate([both[i] for i in order], axis=0)
 
 
-def solve(gram, target):
+def solve(gram, target, between):
     rows = gram.shape[0]
     eye = lax.broadcasted_iota(jnp.int32, gram.shape, 0) == lax.broadcasted_iota(jnp.int32, gram.shape, 1)
-    trace = jnp.sum(
-        jnp.sum(jnp.where(eye, gram, 0.0), axis=0, keepdims=True), axis=1, keepdims=True
-    )
-    unit = 1.0 / (trace / rows)
-    system = gram * unit + jnp.where(eye, 1.0, 0.0)
-    target = target * unit
+    system = gram + jnp.where(eye, 1.0, 0.0)
     first, scales = newton_plan(rows)
     state, solved, path = first * system, first * target, None
     for index, scale in enumerate(scales):
         factor = jnp.where(eye, 2.0 * scale, 0.0) - scale * state
         factor_halves = halves(factor)
-        solved = dot_split(halves(solved), factor_halves)
+        solved = dot_halves(halves(solved), factor_halves)
         if index < len(scales) - 1:
-            state = dot_split(halves(state), factor_halves)
+            state = dot_rows_halved(halves(state), factor_halves)
             if path is None:
                 path = factor_halves[0]
             else:
                 path = jnp.dot(path, factor_halves[0], preferred_element_type=jnp.float32)
                 path = path.astype(jnp.bfloat16)
-    high, low = halves(first * (target - dot_high(solved, system)))
-    step = jnp.dot(high, path, preferred_element_type=jnp.float32)
-    step = step + jnp.dot(low, path, preferred_element_type=jnp.float32)
-    return solved + dot_split(halves(step), factor_halves)
+        between(index)
+    rest = (first * (target - dot_thirds(solved, system))).astype(jnp.bfloat16)
+    step = jnp.dot(rest, path, preferred_element_type=jnp.float32)
+    return solved + dot_halves(halves(step), factor_halves)
 
 
 def fused_kernel(
@@ -124,8 +132,7 @@
     fold_hbm,
     mix_hbm,
     root_out,
-    gram_out,
-    target_out,
+    solved_out,
     grads_out,
     tokens,
     weights,
@@ -175,7 +182,7 @@
     near = z + 1 - 2 * lax.rem(z, 2)
     far = z + 2 - 4 * (z // 2)
     diagonal = near + 2 - 4 * (near // 2)
-    order = (diagonal, near, far, z)
+    order = (diagonal, far, near, z)
     used = []
 
     def load(*pairs):
@@ -219,7 +226,7 @@
     chip_y = chip + 2 - 4 * (chip // 2)
     chip_d = half - 1 - chip
 
-    PAIR, NODE, MID, SIDE, SLICE, ROW, PEER, SUM, SCATTER, ALONG, GATHER, MIX = range(12)
+    PAIR, NODE, MID, LAST, SIDE, SLICE, ROW, PEER, SUM, SCATTER, ALONG, GATHER, MIX = range(13)
 
     def push(phase, source, target, **device):
         pltpu.make_async_remote_copy(
@@ -258,7 +265,10 @@
 
     drain(weights, load_sem.at[weight_load])
     zsend[0] = sides_of_chunk(0)
-    push(MID, zsend.at[0], zmid, tensor=near)
+    token_halves = (slice(0, SEQ // 2), slice(SEQ // 2, SEQ))
+    for phase, span in zip((MID, LAST), token_halves):
+        push(phase, zsend.at[0, span], zmid.at[span], tensor=near)
+    far_sides = sides_of_chunk(1)
 
     drain(order_ref, load_sem.at[order_load])
     drain(prior, load_sem.at[prior_load])
@@ -277,12 +287,12 @@
     for other in (chip_x, chip_y, chip_d):
         push(NODE, node_send.at[other], node_recv.at[chip], dp=2 * other + core)
     node_recv[chip] = node_send[chip]
-    zsend[1] = sides_of_chunk(1)
-    push(SIDE, zsend.at[1], zrecv.at[0], tensor=near)
-    far_sides = sides_of_chunk(2)
-    received(MID, zmid)
-    zsend[2] = far_sides + zmid[...]
-    push(SIDE, zsend.at[2], zrecv.at[1], tensor=far)
+    for phase, span in zip((MID, LAST), token_halves):
+        received(phase, zmid.at[span])
+        zsend[1, span] = far_sides[span] + zmid[span]
+        push(SIDE, zsend.at[1, span], zrecv.at[1, span], tensor=far)
+    zsend[2] = sides_of_chunk(2)
+    push(SIDE, zsend.at[2], zrecv.at[0], tensor=near)
     own_sides = sides_of_chunk(3)
 
     drain(fold_ref, load_sem.at[fold_load])
@@ -314,8 +324,8 @@
     slot = me * n_tp + z
     grads_all[slot] = grads_rows[z * n_dp + me]
     pl.semaphore_wait(ready_sem, n_dp - 1)
+    exchange_all(ROW, lambda d, t: grads_rows.at[t * n_dp + d], grads_all.at[slot])
     exchange("tensor", SLICE, lambda t: slices_send.at[t], grads.at[z])
-    exchange_all(ROW, lambda d, t: grads_rows.at[t * n_dp + d], grads_all.at[slot])
 
     flags = [
         [order_ref[0, j * 2 ** (level + 1) + 2**level - 1] == 1 for j in range(n_dp >> (level + 1))]
@@ -453,6 +463,7 @@
                 square = square + (term if a == b else 2.0 * term)
             mass = masses[2 * j] + masses[2 * j + 1]
             scale = jnp.sqrt(mass / (jnp.maximum(square, 0.0) + 1e-06))
+            trace = scale * scale * square
             new_masses.append(mass)
             new_scales.append([scale * c for c in coefs])
         masses, scales = new_masses, new_scales
@@ -468,6 +479,7 @@
     chunk_halves = halves(jnp.concatenate(chunks, axis=1))
     upper_halves, lower_halves = [[v[s] for v in chunk_halves] for s in (slice(0, LANES), slice(LANES, rows))]
     targets = dot_flip_halves(every_halves, chunk_halves)
+    unit = rows / trace
     triangle = jnp.concatenate(
         [
             dot_flip_halves(chunk_halves, upper_halves),
@@ -478,7 +490,7 @@
         axis=0,
     )
     for r in range(n_dp):
-        gram_part[r] = triangle[r * part_rows : (r + 1) * part_rows]
+        gram_part[r] = unit * triangle[r * part_rows : (r + 1) * part_rows]
     gram_rs[chip] = gram_part[me]
     for other in (chip_d, chip_x, chip_y):
         push(SCATTER, gram_part.at[2 * other + core], gram_rs.at[chip], dp=2 * other + core)
@@ -507,28 +519,23 @@
         part = part + gram_rs[index]
     gram_z[z] = part
     exchange("tensor", ALONG, lambda t: gram_z.at[z], gram_z.at[z])
+    received(ALONG, gram_z.at[: n_tp - 1])
+    part = gram_z[0]
+    for index in range(1, n_tp):
+        part = part + gram_z[index]
+    gram_all[me] = part
+    exchange("dp", GATHER, lambda t: gram_all.at[me], gram_all.at[me])
     relayed(0, 1)
     relay(2, dev_x, dev_y, upper)
     relay(4, dev_x, partner)
     relayed(1, 1)
     relay(3, dev_y, dev_x, lower)
     relay(4, dev_y, partner)
-    received(ALONG, gram_z.at[: n_tp - 1])
-    part = gram_z[0]
-    for index in range(1, n_tp):
-        part = part + gram_z[index]
-    gram_all[me] = part
-    exchange("dp", GATHER, lambda t: gram_all.at[me], gram_all.at[me])
-    relayed(2, 0)
-    relayed(3, 0)
-    relay(4, dev_d, partner)
-    relayed(4, half - 1)
-    root_write = pltpu.make_async_copy(root, root_out, out_sem.at[0])
-    root_write.start()
     for phase, ref in (
         (PAIR, pair_in),
         (NODE, node_recv.at[: half - 1]),
-        (MID, zmid),
+        (MID, zmid.at[: SEQ // 2]),
+        (LAST, zmid.at[SEQ // 2 :]),
         (SIDE, zrecv),
         (SLICE, grads.at[: n_tp - 1]),
         (ROW, grads_all.at[: n_tp * n_dp - 1]),
@@ -541,33 +548,40 @@
         drain(ref, sems.at[0, phase])
     received(GATHER, gram_all.at[: n_dp - 1])
     triangle = jnp.concatenate([gram_all[r] for r in range(n_dp)], axis=0)
-    gram_out[...] = triangle[: rows + LANES]
+    corner = triangle[LANES:rows]
+    gram = jnp.concatenate(
+        [
+            jnp.concatenate([triangle[:LANES], corner.T], axis=1),
+            jnp.concatenate([corner, triangle[rows : rows + LANES]], axis=1),
+        ],
+        axis=0,
+    )
     targets = triangle[rows + LANES :]
     target = jnp.zeros((n_tp, rows), f32)
     for r in range(n_dp):
         span = slice(r * n_tp, (r + 1) * n_tp)
         both = [targets[: n_dp * n_tp][span], targets[n_dp * n_tp :][span]]
         target = jnp.where(me == r, jnp.concatenate(both, axis=1), target)
-    target_out[...] = target
+
+    def between(index):
+        if index == 2:
+            relayed(2, 0)
+            relayed(3, 0)
+            relay(4, dev_d, partner)
+
+    solved_out[...] = solve(gram, target, between)
     drain(gram_all.at[: n_dp - 1], sems.at[0, GATHER])
+    relayed(4, half - 1)
+    root_write = pltpu.make_async_copy(root, root_out, out_sem.at[0])
+    root_write.start()
     drain(root.at[:, : (n_dp - 2) * LANES], root_sems.at[5])
     root_write.wait()
 
 
-def last_kernel(root_ref, gram_ref, target_ref, grads_ref, root_out, pre_out, pre, sem):
+def last_kernel(root_ref, solved_ref, grads_ref, root_out, pre_out, pre, sem):
     write = pltpu.make_async_copy(root_ref, root_out, sem.at[0])
     write.start()
-    rows = root_ref.shape[0]
-    corner = gram_ref[LANES:rows]
-    gram = jnp.concatenate(
-        [
-            jnp.concatenate([gram_ref[:LANES], corner.T], axis=1),
-            jnp.concatenate([corner, gram_ref[rows:]], axis=1),
-        ],
-        axis=0,
-    )
-    solved = solve(gram, target_ref[...])
-    pre[...] = grads_ref[...] - dot_mid(solved, root_ref[...])
+    pre[...] = grads_ref[...] - dot_mid(solved_ref[...], root_ref[...])
     pre_write = pltpu.make_async_copy(pre, pre_out, sem.at[1])
     pre_write.start()
     write.wait()
@@ -597,16 +611,15 @@
     devices = n_dp * n_tp
     part_rows = (3 * LANES + 2 * n_dp * slots) // n_dp
     pin = functools.partial(pltpu.with_memory_space_constraint, memory_space=pltpu.HBM)
-    root, gram, target, grads = pl.pallas_call(
+    root, solved, grads = pl.pallas_call(
         functools.partial(fused_kernel, n_dp, n_tp),
         out_shape=(
             jax.ShapeDtypeStruct((rows, columns), f32),
-            jax.ShapeDtypeStruct((3 * LANES, LANES), f32),
             jax.ShapeDtypeStruct((slots, rows), f32),
             jax.ShapeDtypeStruct((slots, columns), f32),
         ),
         in_specs=[hbm, hbm, hbm, hbm, smem, hbm, hbm, hbm, hbm],
-        out_specs=(anywhere, vmem, vmem, vmem),
+        out_specs=(anywhere, vmem, vmem),
         scratch_shapes=[
             pltpu.VMEM((slots, SEQ, width + hidden), bf16),
             pltpu.VMEM((RANK, width + hidden), bf16),
@@ -635,7 +648,7 @@
             pltpu.VMEM((n_tp, part_rows, LANES), f32),
             pltpu.VMEM((n_dp, part_rows, LANES), f32),
             pltpu.SemaphoreType.DMA((9,)),
-            pltpu.SemaphoreType.DMA((2, 12)),
+            pltpu.SemaphoreType.DMA((2, 13)),
             pltpu.SemaphoreType.DMA((6,)),
             pltpu.SemaphoreType.DMA((1,)),
             pltpu.SemaphoreType.REGULAR,
@@ -660,11 +673,11 @@
             jax.ShapeDtypeStruct((rows, columns), f32),
             jax.ShapeDtypeStruct((slots, columns), f32),
         ),
-        in_specs=[vmem] * 4,
+        in_specs=[vmem] * 3,
         out_specs=(anywhere, anywhere),
         scratch_shapes=[pltpu.VMEM((slots, columns), f32), pltpu.SemaphoreType.DMA((2,))],
         compiler_params=pltpu.CompilerParams(vmem_limit_bytes=16 * 2**20),
-    )(root, gram, target, grads)
+    )(root, solved, grads)
 
 
 def from_partner(value, axis, stride):

time: 42.9 us -> 42.3 us (0.986)
  Pallas kernels: 41.5 us -> 40.9 us
    pallas_call x1, Pallas kernels: 4.32 us -> 0.99 us  [fused_body(): pl.pallas_call(last_kernel, out_shape=(jax.ShapeDtypeStruct((rows, column...]
    pallas_call x1, Pallas kernels: 37.2 us -> 39.9 us  [fused_body(): pl.pallas_call(functools.partial(fused_kernel, n_dp, n_tp), out_shape=(ja...]
where the time goes in v4:
time: 42.3 us; the launch traced here: 42.2 us
  Pallas kernels  40.9 us (97%)
  between operations  1.29 us (3%)
    pallas_call x1, Pallas kernels, fused_body(): pl.pallas_call(functools.partial(fused_kernel, n_dp, n_tp), out_shape=(ja...  39.9 us
    pallas_call x1, Pallas kernels, fused_body(): pl.pallas_call(last_kernel, out_shape=(jax.ShapeDtypeStruct((rows, column...  0.99 us

profile of v4, /device:TPU:0, one launch (start us, length us, event | category | flops | bytes accessed | tf_op | source)
XLA Modules:
  0.0 42.2 jit_solution(17588880997990606360)
XLA Ops:
  1.3 39.9 %shard_map.104 = (f32[256,1024]{1,0:T(8,128)S(1)}, f32[4,256]{1,0:T(4,128)S(1)}, f32[4,1024]{1,0:T(4,128)S(1)}) custom-call(bf16[512,2048]{1,0:T(8,128)(2,1)} %act_hbm.1, bf16[512,7168]{1,0:T(8,128)(2,1)} %out_hbm.1, bf16[64,2048]{1,0:T(8,128)(2,1)} %bitcast.5, bf16[64,7168]{1,0:T(8,128)(2,1)} %bitcast.4, s32[1]{0:T(128)S(6)} %copy.11.count_ref, ...), custom_call_target="tpu_custom_call" | custom-call | tf_op jit(solution)/shard_map/pallas_call | solution.py:614
  41.2 1.0 %shard_map.105 = (f32[256,1024]{1,0:T(8,128)}, f32[4,1024]{1,0:T(4,128)}) custom-call(f32[256,1024]{1,0:T(8,128)S(1)} %get-tuple-element.5.root_ref, f32[4,256]{1,0:T(4,128)S(1)} %get-tuple-element.6.solved_ref, f32[4,1024]{1,0:T(4,128)S(1)} %get-tuple-element.7.grads_ref), custom_call_target="tpu_custom_call" | custom-call | tf_op jit(solution)/shard_map/pallas_call | solution.py:670

commit v5 on v4

--- a/solution.py
+++ b/solution.py
@@ -76,9 +76,8 @@
 
 
 def thirds(value):
-    high, rest = halves(value)
-    rest = value - high.astype(jnp.float32)
-    return (high, *halves(rest))
+    high = value.astype(jnp.bfloat16)
+    return (high, *halves(value - high.astype(jnp.float32)))
 
 
 def dot_thirds(left, right):
@@ -96,7 +95,7 @@
     return jnp.concatenate([both[i] for i in order], axis=0)
 
 
-def solve(gram, target, between):
+def solve(gram, target):
     rows = gram.shape[0]
     eye = lax.broadcasted_iota(jnp.int32, gram.shape, 0) == lax.broadcasted_iota(jnp.int32, gram.shape, 1)
     system = gram + jnp.where(eye, 1.0, 0.0)
@@ -113,7 +112,6 @@
             else:
                 path = jnp.dot(path, factor_halves[0], preferred_element_type=jnp.float32)
                 path = path.astype(jnp.bfloat16)
-        between(index)
     rest = (first * (target - dot_thirds(solved, system))).astype(jnp.bfloat16)
     step = jnp.dot(rest, path, preferred_element_type=jnp.float32)
     return solved + dot_halves(halves(step), factor_halves)
@@ -268,7 +266,6 @@
     token_halves = (slice(0, SEQ // 2), slice(SEQ // 2, SEQ))
     for phase, span in zip((MID, LAST), token_halves):
         push(phase, zsend.at[0, span], zmid.at[span], tensor=near)
-    far_sides = sides_of_chunk(1)
 
     drain(order_ref, load_sem.at[order_load])
     drain(prior, load_sem.at[prior_load])
@@ -287,6 +284,7 @@
     for other in (chip_x, chip_y, chip_d):
         push(NODE, node_send.at[other], node_recv.at[chip], dp=2 * other + core)
     node_recv[chip] = node_send[chip]
+    far_sides = sides_of_chunk(1)
     for phase, span in zip((MID, LAST), token_halves):
         received(phase, zmid.at[span])
         zsend[1, span] = far_sides[span] + zmid[span]
@@ -324,8 +322,8 @@
     slot = me * n_tp + z
     grads_all[slot] = grads_rows[z * n_dp + me]
     pl.semaphore_wait(ready_sem, n_dp - 1)
+    exchange("tensor", SLICE, lambda t: slices_send.at[t], grads.at[z])
     exchange_all(ROW, lambda d, t: grads_rows.at[t * n_dp + d], grads_all.at[slot])
-    exchange("tensor", SLICE, lambda t: slices_send.at[t], grads.at[z])
 
     flags = [
         [order_ref[0, j * 2 ** (level + 1) + 2**level - 1] == 1 for j in range(n_dp >> (level + 1))]
@@ -482,7 +480,8 @@
     unit = rows / trace
     triangle = jnp.concatenate(
         [
-            dot_flip_halves(chunk_halves, upper_halves),
+            dot_flip_halves(upper_halves, upper_halves),
+            dot_flip_halves(lower_halves, upper_halves),
             dot_flip_halves(lower_halves, lower_halves),
             targets[:, :LANES],
             targets[:, LANES:],
@@ -519,18 +518,21 @@
         part = part + gram_rs[index]
     gram_z[z] = part
     exchange("tensor", ALONG, lambda t: gram_z.at[z], gram_z.at[z])
+    relayed(0, 1)
+    relay(2, dev_x, dev_y, upper)
+    relay(4, dev_x, partner)
+    relayed(1, 1)
+    relay(3, dev_y, dev_x, lower)
+    relay(4, dev_y, partner)
     received(ALONG, gram_z.at[: n_tp - 1])
     part = gram_z[0]
     for index in range(1, n_tp):
         part = part + gram_z[index]
     gram_all[me] = part
     exchange("dp", GATHER, lambda t: gram_all.at[me], gram_all.at[me])
-    relayed(0, 1)
-    relay(2, dev_x, dev_y, upper)
-    relay(4, dev_x, partner)
-    relayed(1, 1)
-    relay(3, dev_y, dev_x, lower)
-    relay(4, dev_y, partner)
+    relayed(2, 0)
+    relayed(3, 0)
+    relay(4, dev_d, partner)
     for phase, ref in (
         (PAIR, pair_in),
         (NODE, node_recv.at[: half - 1]),
@@ -562,14 +564,7 @@
         span = slice(r * n_tp, (r + 1) * n_tp)
         both = [targets[: n_dp * n_tp][span], targets[n_dp * n_tp :][span]]
         target = jnp.where(me == r, jnp.concatenate(both, axis=1), target)
-
-    def between(index):
-        if index == 2:
-            relayed(2, 0)
-            relayed(3, 0)
-            relay(4, dev_d, partner)
-
-    solved_out[...] = solve(gram, target, between)
+    solved_out[...] = solve(gram, target)
     drain(gram_all.at[: n_dp - 1], sems.at[0, GATHER])
     relayed(4, half - 1)
     root_write = pltpu.make_async_copy(root, root_out, out_sem.at[0])

time: 42.3 us -> 41.7 us (0.986)
  Pallas kernels: 40.9 us -> 40.3 us
    pallas_call x1, Pallas kernels: 39.9 us -> 39.3 us  [fused_body(): pl.pallas_call(functools.partial(fused_kernel, n_dp, n_tp), out_shape=(ja...]
where the time goes in v5:
time: 41.7 us; the launch traced here: 41.5 us
  Pallas kernels  40.3 us (97%)
  between operations  1.29 us (3%)
    pallas_call x1, Pallas kernels, fused_body(): pl.pallas_call(functools.partial(fused_kernel, n_dp, n_tp), out_shape=(ja...  39.3 us
    pallas_call x1, Pallas kernels, fused_body(): pl.pallas_call(last_kernel, out_shape=(jax.ShapeDtypeStruct((rows, column...  0.99 us

profile of v5, /device:TPU:0, one launch (start us, length us, event | category | flops | bytes accessed | tf_op | source)
XLA Modules:
  0.0 41.5 jit_solution(9844656254152117493)
XLA Ops:
  1.3 39.3 %shard_map.104 = (f32[256,1024]{1,0:T(8,128)S(1)}, f32[4,256]{1,0:T(4,128)S(1)}, f32[4,1024]{1,0:T(4,128)S(1)}) custom-call(bf16[512,2048]{1,0:T(8,128)(2,1)} %act_hbm.1, bf16[512,7168]{1,0:T(8,128)(2,1)} %out_hbm.1, bf16[64,2048]{1,0:T(8,128)(2,1)} %bitcast.5, bf16[64,7168]{1,0:T(8,128)(2,1)} %bitcast.4, s32[1]{0:T(128)S(6)} %copy.11.count_ref, ...), custom_call_target="tpu_custom_call" | custom-call | tf_op jit(solution)/shard_map/pallas_call | solution.py:609
  40.6 1.0 %shard_map.105 = (f32[256,1024]{1,0:T(8,128)}, f32[4,1024]{1,0:T(4,128)}) custom-call(f32[256,1024]{1,0:T(8,128)S(1)} %get-tuple-element.5.root_ref, f32[4,256]{1,0:T(4,128)S(1)} %get-tuple-element.6.solved_ref, f32[4,1024]{1,0:T(4,128)S(1)} %get-tuple-element.7.grads_ref), custom_call_target="tpu_custom_call" | custom-call | tf_op jit(solution)/shard_map/pallas_call | solution.py:665

commit v6 on v5

--- a/solution.py
+++ b/solution.py
@@ -32,12 +32,6 @@
 
 def dot_flip(left, right):
     return lax.dot_general(left, right, (((1,), (1,)), ((), ())), preferred_element_type=jnp.float32)
-
-
-def dot_rows(left, right):
-    return lax.dot_general(
-        left, right, (((1,), (1,)), ((), ())), precision=HIGHEST, preferred_element_type=jnp.float32
-    )
 
 
 def halves(value):
@@ -224,7 +218,7 @@
     chip_y = chip + 2 - 4 * (chip // 2)
     chip_d = half - 1 - chip
 
-    PAIR, NODE, MID, LAST, SIDE, SLICE, ROW, PEER, SUM, SCATTER, ALONG, GATHER, MIX = range(13)
+    PAIR, NODE, MID, SIDE, SLICE, ROW, PEER, SUM, SCATTER, ALONG, GATHER, MIX = range(12)
 
     def push(phase, source, target, **device):
         pltpu.make_async_remote_copy(
@@ -259,13 +253,15 @@
         spans = [slice(h * mid, (h + 1) * mid) for h in range(2)]
         right = [dot_flip(tokens[index, span, width:], weights[:, width:]) for span in spans]
         left = [dot_flip(tokens[index, span, :width], weights[:, :width]) for span in spans]
-        return jnp.concatenate([jnp.concatenate(pair, axis=1) for pair in zip(left, right)], axis=0)
+        return [jnp.concatenate(pair, axis=1) for pair in zip(left, right)]
 
     drain(weights, load_sem.at[weight_load])
-    zsend[0] = sides_of_chunk(0)
-    token_halves = (slice(0, SEQ // 2), slice(SEQ // 2, SEQ))
-    for phase, span in zip((MID, LAST), token_halves):
-        push(phase, zsend.at[0, span], zmid.at[span], tensor=near)
+    zsend[0], zsend[1] = sides_of_chunk(0)
+    push(MID, zsend.at[0], zmid, tensor=near)
+    push(SIDE, zsend.at[1], zrecv.at[4], tensor=diagonal)
+    far_sides = sides_of_chunk(1)
+    zsend[3] = far_sides[1]
+    push(SIDE, zsend.at[3], zrecv.at[3], tensor=far)
 
     drain(order_ref, load_sem.at[order_load])
     drain(prior, load_sem.at[prior_load])
@@ -284,27 +280,42 @@
     for other in (chip_x, chip_y, chip_d):
         push(NODE, node_send.at[other], node_recv.at[chip], dp=2 * other + core)
     node_recv[chip] = node_send[chip]
-    far_sides = sides_of_chunk(1)
-    for phase, span in zip((MID, LAST), token_halves):
-        received(phase, zmid.at[span])
-        zsend[1, span] = far_sides[span] + zmid[span]
-        push(SIDE, zsend.at[1, span], zrecv.at[1, span], tensor=far)
-    zsend[2] = sides_of_chunk(2)
-    push(SIDE, zsend.at[2], zrecv.at[0], tensor=near)
+    received(MID, zmid)
+    zsend[2] = far_sides[0] + zmid[...]
+    push(SIDE, zsend.at[2], zrecv.at[2], tensor=far)
+    zsend[4], zsend[5] = sides_of_chunk(2)
+    push(SIDE, zsend.at[4:6], zrecv.at[0:2], tensor=near)
     own_sides = sides_of_chunk(3)
 
     drain(fold_ref, load_sem.at[fold_load])
     fold_rows = fold_ref[...]
-    paths = [[jnp.concatenate([dot_rows(fold_rows, first_mix), dot_rows(fold_rows, second_mix)], axis=0)]]
+
+    def through(value):
+        count = value.shape[0]
+        both = stacked(value, (0, 1)).astype(jnp.bfloat16)
+        high = value.astype(jnp.bfloat16)
+        results = []
+        for top, bottom in (first_halves, second_halves):
+            most = dot_flip(both, top)
+            results.append(most[:count] + (most[count:] + dot_flip(high, bottom)))
+        return results
+
+    paths = [[jnp.concatenate(through(fold_rows), axis=0)]]
     for level in range(1, levels):
-        paths.append(
-            [dot_rows(p, first_mix) for p in paths[-1]] + [dot_rows(p, second_mix) for p in paths[-1]]
-        )
+        count = paths[-1][0].shape[0]
+        mapped = through(jnp.concatenate(paths[-1], axis=0))
+        paths.append([v[i : i + count] for v in mapped for i in range(0, v.shape[0], count)])
     paths = [[stacked(p, (0, 0, 1)).T.astype(jnp.bfloat16) for p in level] for level in paths]
     fold = fold_rows.T
 
     received(SIDE, zrecv)
-    sides = (own_sides + zrecv[0]) + zrecv[1]
+    sides = jnp.concatenate(
+        [
+            (own_sides[0] + zrecv[0]) + zrecv[2],
+            (own_sides[1] + zrecv[1]) + (zrecv[3] + zrecv[4]),
+        ],
+        axis=0,
+    )
     lane = lax.broadcasted_iota(jnp.int32, sides.shape, 1)
     doubled = jnp.where(lane < RANK, sides, pltpu.roll(sides, RANK, 1))
     product = dot_mid(sides.T, doubled) / jnp.sqrt(f32(SEQ))
@@ -536,8 +547,7 @@
     for phase, ref in (
         (PAIR, pair_in),
         (NODE, node_recv.at[: half - 1]),
-        (MID, zmid.at[: SEQ // 2]),
-        (LAST, zmid.at[SEQ // 2 :]),
+        (MID, zmid),
         (SIDE, zrecv),
         (SLICE, grads.at[: n_tp - 1]),
         (ROW, grads_all.at[: n_tp * n_dp - 1]),
@@ -625,9 +635,9 @@
             pltpu.VMEM((n_dp // 2, rows, LANES), f32),
             pltpu.VMEM((n_dp // 2, rows, LANES), f32),
             pltpu.VMEM((n_dp // 2, rows, LANES), f32),
-            pltpu.VMEM((3, SEQ, LANES), f32),
-            pltpu.VMEM((SEQ, LANES), f32),
-            pltpu.VMEM((2, SEQ, LANES), f32),
+            pltpu.VMEM((6, SEQ // 2, LANES), f32),
+            pltpu.VMEM((SEQ // 2, LANES), f32),
+            pltpu.VMEM((5, SEQ // 2, LANES), f32),
             pltpu.VMEM((RANK, LANES), f32),
             pltpu.VMEM((n_tp, n_dp, LANES), f32),
             pltpu.VMEM((n_tp, n_dp, LANES), f32),
@@ -643,7 +653,7 @@
             pltpu.VMEM((n_tp, part_rows, LANES), f32),
             pltpu.VMEM((n_dp, part_rows, LANES), f32),
             pltpu.SemaphoreType.DMA((9,)),
-            pltpu.SemaphoreType.DMA((2, 13)),
+            pltpu.SemaphoreType.DMA((2, 12)),
             pltpu.SemaphoreType.DMA((6,)),
             pltpu.SemaphoreType.DMA((1,)),
             pltpu.SemaphoreType.REGULAR,

time: 41.7 us -> 40.9 us (0.981)
  Pallas kernels: 40.3 us -> 39.4 us
    pallas_call x1, Pallas kernels: 39.3 us -> 38.4 us  [fused_body(): pl.pallas_call(functools.partial(fused_kernel, n_dp, n_tp), out_shape=(ja...]
where the time goes in v6:
time: 40.9 us; the launch traced here: 40.7 us
  Pallas kernels  39.4 us (96%)
  between operations  1.29 us (3%)
    pallas_call x1, Pallas kernels, fused_body(): pl.pallas_call(functools.partial(fused_kernel, n_dp, n_tp), out_shape=(ja...  38.4 us
    pallas_call x1, Pallas kernels, fused_body(): pl.pallas_call(last_kernel, out_shape=(jax.ShapeDtypeStruct((rows, column...  0.99 us

profile of v6, /device:TPU:0, one launch (start us, length us, event | category | flops | bytes accessed | tf_op | source)
XLA Modules:
  0.0 40.7 jit_solution(16077720509185172324)
XLA Ops:
  1.3 38.4 %shard_map.104 = (f32[256,1024]{1,0:T(8,128)S(1)}, f32[4,256]{1,0:T(4,128)S(1)}, f32[4,1024]{1,0:T(4,128)S(1)}) custom-call(bf16[512,2048]{1,0:T(8,128)(2,1)} %act_hbm.1, bf16[512,7168]{1,0:T(8,128)(2,1)} %out_hbm.1, bf16[64,2048]{1,0:T(8,128)(2,1)} %bitcast.5, bf16[64,7168]{1,0:T(8,128)(2,1)} %bitcast.4, s32[1]{0:T(128)S(6)} %copy.11.count_ref, ...), custom_call_target="tpu_custom_call" | custom-call | tf_op jit(solution)/shard_map/pallas_call | solution.py:619
  39.7 1.0 %shard_map.105 = (f32[256,1024]{1,0:T(8,128)}, f32[4,1024]{1,0:T(4,128)}) custom-call(f32[256,1024]{1,0:T(8,128)S(1)} %get-tuple-element.5.root_ref, f32[4,256]{1,0:T(4,128)S(1)} %get-tuple-element.6.solved_ref, f32[4,1024]{1,0:T(4,128)S(1)} %get-tuple-element.7.grads_ref), custom_call_target="tpu_custom_call" | custom-call | tf_op jit(solution)/shard_map/pallas_call | solution.py:675

commit v7 on v6

--- a/solution.py
+++ b/solution.py
@@ -161,7 +161,6 @@
     f32 = jnp.float32
     me, z = lax.axis_index("dp"), lax.axis_index("tensor")
     rows = prior.shape[0]
-    part_rows = gram_z.shape[1]
     levels = n_dp.bit_length() - 1
 
     def dp_of(k):
@@ -207,9 +206,6 @@
         pl.semaphore_signal(barrier, inc=1, device_id={"tensor": tp_of(k)}, device_id_type=MESH)
     for k in range(1, n_dp):
         pl.semaphore_signal(barrier, inc=1, device_id={"dp": dp_of(k)}, device_id_type=MESH)
-    pl.semaphore_wait(barrier, n_dp + n_tp - 2)
-    for k in range(1, n_dp):
-        pl.semaphore_signal(ready_sem, inc=1, device_id={"dp": dp_of(k)}, device_id_type=MESH)
 
     half = n_dp // 2
     core, chip = lax.rem(me, 2), me // 2
@@ -233,9 +229,6 @@
     def received(phase, ref):
         drain(ref, sems.at[1, phase])
 
-    for q in range(half):
-        push(PAIR, prior_hbm.at[:, tile_of(2 * q + 1 - core)], pair_in.at[q], dp=partner)
-
     def exchange(axis, phase, source, target):
         size, other = (n_tp, tp_of) if axis == "tensor" else (n_dp, dp_of)
         for k in range(1, size):
@@ -257,11 +250,18 @@
 
     drain(weights, load_sem.at[weight_load])
     zsend[0], zsend[1] = sides_of_chunk(0)
+    pl.semaphore_wait(barrier, n_dp + n_tp - 2)
     push(MID, zsend.at[0], zmid, tensor=near)
     push(SIDE, zsend.at[1], zrecv.at[4], tensor=diagonal)
+    for q in range(half):
+        push(PAIR, prior_hbm.at[:, tile_of(2 * q + 1 - core)], pair_in.at[q], dp=partner)
+    for k in range(1, n_dp):
+        pl.semaphore_signal(ready_sem, inc=1, device_id={"dp": dp_of(k)}, device_id_type=MESH)
     far_sides = sides_of_chunk(1)
     zsend[3] = far_sides[1]
     push(SIDE, zsend.at[3], zrecv.at[3], tensor=far)
+    zsend[4], zsend[5] = sides_of_chunk(2)
+    push(SIDE, zsend.at[4:6], zrecv.at[0:2], tensor=near)
 
     drain(order_ref, load_sem.at[order_load])
     drain(prior, load_sem.at[prior_load])
@@ -283,8 +283,6 @@
     received(MID, zmid)
     zsend[2] = far_sides[0] + zmid[...]
     push(SIDE, zsend.at[2], zrecv.at[2], tensor=far)
-    zsend[4], zsend[5] = sides_of_chunk(2)
-    push(SIDE, zsend.at[4:6], zrecv.at[0:2], tensor=near)
     own_sides = sides_of_chunk(3)
 
     drain(fold_ref, load_sem.at[fold_load])
@@ -348,6 +346,17 @@
     def total(value):
         return jnp.sum(jnp.sum(value, axis=0, keepdims=True), axis=1, keepdims=True)
 
+    received(SLICE, grads.at[: n_tp - 1])
+    leaf_square = jnp.zeros((rows, LANES), f32)
+    for tile in range(n_dp):
+        leaf = prior[:, tile * LANES : (tile + 1) * LANES]
+        for e in range(n_tp):
+            step = grads[e, tile : tile + 1, :]
+            grads_out[e : e + 1, tile * LANES : (tile + 1) * LANES] = step
+            leaf = leaf + fold[:, e : e + 1] * step
+        leaf_square = leaf_square + leaf * leaf
+    own_mass = total(leaf_square)
+
     received(NODE, node_recv.at[: half - 1])
     mixtures = [[[node_recv[j]] for j in range(half)]]
     for level in range(1, levels):
@@ -370,17 +379,6 @@
     for index, part in enumerate(mixtures[-1][0]):
         mix_send[index] = part
     push(MIX, mix_send, mix_recv, dp=partner)
-
-    received(SLICE, grads.at[: n_tp - 1])
-    leaf_square = jnp.zeros((rows, LANES), f32)
-    for tile in range(n_dp):
-        leaf = prior[:, tile * LANES : (tile + 1) * LANES]
-        for e in range(n_tp):
-            step = grads[e, tile : tile + 1, :]
-            grads_out[e : e + 1, tile * LANES : (tile + 1) * LANES] = step
-            leaf = leaf + fold[:, e : e + 1] * step
-        leaf_square = leaf_square + leaf * leaf
-    own_mass = total(leaf_square)
 
     received(ROW, grads_all.at[: n_tp * n_dp - 1])
     push(PEER, grads_all, peer_all, dp=partner)
@@ -494,13 +492,14 @@
             dot_flip_halves(upper_halves, upper_halves),
             dot_flip_halves(lower_halves, upper_halves),
             dot_flip_halves(lower_halves, lower_halves),
-            targets[:, :LANES],
-            targets[:, LANES:],
         ],
         axis=0,
     )
+    own_rows = gram_all.shape[1]
     for r in range(n_dp):
-        gram_part[r] = unit * triangle[r * part_rows : (r + 1) * part_rows]
+        gram_part[r, :own_rows] = unit * triangle[r * own_rows : (r + 1) * own_rows]
+        own = targets[r * n_tp : (r + 1) * n_tp]
+        gram_part[r, own_rows:] = unit * jnp.concatenate([own[:, :LANES], own[:, LANES:]], axis=0)
     gram_rs[chip] = gram_part[me]
     for other in (chip_d, chip_x, chip_y):
         push(SCATTER, gram_part.at[2 * other + core], gram_rs.at[chip], dp=2 * other + core)
@@ -521,6 +520,7 @@
     def relayed(index, count):
         drain(root.at[:, : count * LANES] if count else root.at[upper, :LANES], root_sems.at[index])
 
+    drain(gram_rs.at[: half - 1], sems.at[0, SCATTER])
     relay(0, me, dev_x)
     relay(1, me, dev_y)
     received(SCATTER, gram_rs.at[: half - 1])
@@ -539,7 +539,8 @@
     part = gram_z[0]
     for index in range(1, n_tp):
         part = part + gram_z[index]
-    gram_all[me] = part
+    gram_all[me] = part[:own_rows]
+    target = jnp.concatenate([part[own_rows : own_rows + n_tp], part[own_rows + n_tp :]], axis=1)
     exchange("dp", GATHER, lambda t: gram_all.at[me], gram_all.at[me])
     relayed(2, 0)
     relayed(3, 0)
@@ -554,7 +555,6 @@
         (SUM, sums_all.at[: n_tp * n_dp - 1]),
         (PEER, peer_all),
         (MIX, mix_recv),
-        (SCATTER, gram_rs.at[: half - 1]),
         (ALONG, gram_z.at[: n_tp - 1]),
     ):
         drain(ref, sems.at[0, phase])
@@ -568,12 +568,6 @@
         ],
         axis=0,
     )
-    targets = triangle[rows + LANES :]
-    target = jnp.zeros((n_tp, rows), f32)
-    for r in range(n_dp):
-        span = slice(r * n_tp, (r + 1) * n_tp)
-        both = [targets[: n_dp * n_tp][span], targets[n_dp * n_tp :][span]]
-        target = jnp.where(me == r, jnp.concatenate(both, axis=1), target)
     solved_out[...] = solve(gram, target)
     drain(gram_all.at[: n_dp - 1], sems.at[0, GATHER])
     relayed(4, half - 1)
@@ -614,7 +608,8 @@
     vmem = pl.BlockSpec(memory_space=pltpu.VMEM)
     smem = pl.BlockSpec(memory_space=pltpu.SMEM)
     devices = n_dp * n_tp
-    part_rows = (3 * LANES + 2 * n_dp * slots) // n_dp
+    own_rows = 3 * LANES // n_dp
+    part_rows = own_rows + 2 * slots
     pin = functools.partial(pltpu.with_memory_space_constraint, memory_space=pltpu.HBM)
     root, solved, grads = pl.pallas_call(
         functools.partial(fused_kernel, n_dp, n_tp),
@@ -651,7 +646,7 @@
             pltpu.VMEM((n_dp, part_rows, LANES), f32),
             pltpu.VMEM((n_dp // 2, part_rows, LANES), f32),
             pltpu.VMEM((n_tp, part_rows, LANES), f32),
-            pltpu.VMEM((n_dp, part_rows, LANES), f32),
+            pltpu.VMEM((n_dp, own_rows, LANES), f32),
             pltpu.SemaphoreType.DMA((9,)),
             pltpu.SemaphoreType.DMA((2, 12)),
             pltpu.SemaphoreType.DMA((6,)),
@@ -761,7 +756,6 @@
         and n_dp == 8
         and n_tp == 4
         and rows == 2 * LANES
-        and (3 * LANES + 2 * n_dp * slots) % (8 * n_dp) == 0
     )
 
 

time: 40.9 us -> 39.6 us (0.968)
  Pallas kernels: 39.4 us -> 38.2 us
    pallas_call x1, Pallas kernels: 38.4 us -> 37.2 us  [fused_body(): pl.pallas_call(functools.partial(fused_kernel, n_dp, n_tp), out_shape=(ja...]
where the time goes in v7:
time: 39.6 us; the launch traced here: 39.5 us
  Pallas kernels  38.2 us (96%)
  between operations  1.29 us (3%)
    pallas_call x1, Pallas kernels, fused_body(): pl.pallas_call(functools.partial(fused_kernel, n_dp, n_tp), out_shape=(ja...  37.2 us
    pallas_call x1, Pallas kernels, fused_body(): pl.pallas_call(last_kernel, out_shape=(jax.ShapeDtypeStruct((rows, column...  0.99 us

profile of v7, /device:TPU:0, one launch (start us, length us, event | category | flops | bytes accessed | tf_op | source)
XLA Modules:
  0.0 39.5 jit_solution(6629667150289194829)
XLA Ops:
  1.3 37.2 %shard_map.104 = (f32[256,1024]{1,0:T(8,128)S(1)}, f32[4,256]{1,0:T(4,128)S(1)}, f32[4,1024]{1,0:T(4,128)S(1)}) custom-call(bf16[512,2048]{1,0:T(8,128)(2,1)} %act_hbm.1, bf16[512,7168]{1,0:T(8,128)(2,1)} %out_hbm.1, bf16[64,2048]{1,0:T(8,128)(2,1)} %bitcast.5, bf16[64,7168]{1,0:T(8,128)(2,1)} %bitcast.4, s32[1]{0:T(128)S(6)} %copy.11.count_ref, ...), custom_call_target="tpu_custom_call" | custom-call | tf_op jit(solution)/shard_map/pallas_call | solution.py:614
  38.5 1.0 %shard_map.105 = (f32[256,1024]{1,0:T(8,128)}, f32[4,1024]{1,0:T(4,128)}) custom-call(f32[256,1024]{1,0:T(8,128)S(1)} %get-tuple-element.5.root_ref, f32[4,256]{1,0:T(4,128)S(1)} %get-tuple-element.6.solved_ref, f32[4,1024]{1,0:T(4,128)S(1)} %get-tuple-element.7.grads_ref), custom_call_target="tpu_custom_call" | custom-call | tf_op jit(solution)/shard_map/pallas_call | solution.py:670

commit v8 on v7

--- a/solution.py
+++ b/solution.py
@@ -185,17 +185,18 @@
     def drain(ref, sem):
         pltpu.make_async_copy(ref, ref, sem).wait()
 
-    def load_chunk(index):
-        span = pl.ds(pl.multiple_of(order[index] * SEQ, SEQ), SEQ)
-        into = tokens.at[index]
+    def load_chunk(index, start=0, count=SEQ):
+        span = pl.ds(pl.multiple_of(order[index] * SEQ + start, count), count)
+        into = tokens.at[index, start : start + count]
         return load((act_hbm.at[span], into.at[:, :width]), (out_hbm.at[span], into.at[:, width:]))
 
     order_load = load((order_hbm, order_ref))
     weight_load = load((wi_hbm, weights.at[:, :width]), (wo_hbm, weights.at[:, width:]))
-    chunk_loads = [load_chunk(0)]
+    mid = SEQ // 2
+    half_loads = [load_chunk(0, start, mid) for start in (0, mid)]
     prior_load = load((prior_hbm, prior))
     mix_load = load((mix_hbm, mix_ref))
-    chunk_loads += [load_chunk(index) for index in range(1, n_tp)]
+    chunk_loads = [None] + [load_chunk(index) for index in range(1, n_tp)]
     fold_load = load((fold_hbm, fold_ref))
 
     def tile_of(owner):
@@ -240,23 +241,30 @@
                 if (j, k) != (0, 0):
                     push(phase, source(dp_of(k), tp_of(j)), target, dp=dp_of(k), tensor=tp_of(j))
 
-    def sides_of_chunk(index):
-        drain(tokens.at[index], load_sem.at[chunk_loads[index]])
-        mid = SEQ // 2
-        spans = [slice(h * mid, (h + 1) * mid) for h in range(2)]
+    def sides_of_rows(index, start, count):
+        spans = [slice(start + h * count, start + (h + 1) * count) for h in range(2)]
         right = [dot_flip(tokens[index, span, width:], weights[:, width:]) for span in spans]
         left = [dot_flip(tokens[index, span, :width], weights[:, :width]) for span in spans]
         return [jnp.concatenate(pair, axis=1) for pair in zip(left, right)]
 
+    def sides_of_chunk(index):
+        drain(tokens.at[index], load_sem.at[chunk_loads[index]])
+        return sides_of_rows(index, 0, mid)
+
+    def sides_of_half(h):
+        drain(tokens.at[0, h * mid : (h + 1) * mid], load_sem.at[half_loads[h]])
+        zsend[h] = jnp.concatenate(sides_of_rows(0, h * mid, mid // 2), axis=0)
+
     drain(weights, load_sem.at[weight_load])
-    zsend[0], zsend[1] = sides_of_chunk(0)
+    sides_of_half(0)
     pl.semaphore_wait(barrier, n_dp + n_tp - 2)
     push(MID, zsend.at[0], zmid, tensor=near)
-    push(SIDE, zsend.at[1], zrecv.at[4], tensor=diagonal)
     for q in range(half):
         push(PAIR, prior_hbm.at[:, tile_of(2 * q + 1 - core)], pair_in.at[q], dp=partner)
     for k in range(1, n_dp):
         pl.semaphore_signal(ready_sem, inc=1, device_id={"dp": dp_of(k)}, device_id_type=MESH)
+    sides_of_half(1)
+    push(SIDE, zsend.at[1], zrecv.at[4], tensor=diagonal)
     far_sides = sides_of_chunk(1)
     zsend[3] = far_sides[1]
     push(SIDE, zsend.at[3], zrecv.at[3], tensor=far)
@@ -647,7 +655,7 @@
             pltpu.VMEM((n_dp // 2, part_rows, LANES), f32),
             pltpu.VMEM((n_tp, part_rows, LANES), f32),
             pltpu.VMEM((n_dp, own_rows, LANES), f32),
-            pltpu.SemaphoreType.DMA((9,)),
+            pltpu.SemaphoreType.DMA((10,)),
             pltpu.SemaphoreType.DMA((2, 12)),
             pltpu.SemaphoreType.DMA((6,)),
             pltpu.SemaphoreType.DMA((1,)),

time: 39.6 us -> 39.5 us (level)
  no operation moved by 1% of the time
where the time goes in v8:
time: 39.5 us; the launch traced here: 39.3 us
  Pallas kernels  38 us (96%)
  between operations  1.29 us (3%)
    pallas_call x1, Pallas kernels, fused_body(): pl.pallas_call(functools.partial(fused_kernel, n_dp, n_tp), out_shape=(ja...  37 us
    pallas_call x1, Pallas kernels, fused_body(): pl.pallas_call(last_kernel, out_shape=(jax.ShapeDtypeStruct((rows, column...  0.99 us

profile of v8, /device:TPU:0, one launch (start us, length us, event | category | flops | bytes accessed | tf_op | source)
XLA Modules:
  0.0 39.3 jit_solution(7494974745170542109)
XLA Ops:
  1.3 37.0 %shard_map.104 = (f32[256,1024]{1,0:T(8,128)S(1)}, f32[4,256]{1,0:T(4,128)S(1)}, f32[4,1024]{1,0:T(4,128)S(1)}) custom-call(bf16[512,2048]{1,0:T(8,128)(2,1)} %act_hbm.1, bf16[512,7168]{1,0:T(8,128)(2,1)} %out_hbm.1, bf16[64,2048]{1,0:T(8,128)(2,1)} %bitcast.5, bf16[64,7168]{1,0:T(8,128)(2,1)} %bitcast.4, s32[1]{0:T(128)S(6)} %copy.11.count_ref, ...), custom_call_target="tpu_custom_call" | custom-call | tf_op jit(solution)/shard_map/pallas_call | solution.py:622
  38.3 1.0 %shard_map.105 = (f32[256,1024]{1,0:T(8,128)}, f32[4,1024]{1,0:T(4,128)}) custom-call(f32[256,1024]{1,0:T(8,128)S(1)} %get-tuple-element.5.root_ref, f32[4,256]{1,0:T(4,128)S(1)} %get-tuple-element.6.solved_ref, f32[4,1024]{1,0:T(4,128)S(1)} %get-tuple-element.7.grads_ref), custom_call_target="tpu_custom_call" | custom-call | tf_op jit(solution)/shard_map/pallas_call | solution.py:678

commit v9 on v8

--- a/solution.py
+++ b/solution.py
@@ -312,7 +312,25 @@
         mapped = through(jnp.concatenate(paths[-1], axis=0))
         paths.append([v[i : i + count] for v in mapped for i in range(0, v.shape[0], count)])
     paths = [[stacked(p, (0, 0, 1)).T.astype(jnp.bfloat16) for p in level] for level in paths]
-    fold = fold_rows.T
+    def total(value):
+        return jnp.sum(jnp.sum(value, axis=0, keepdims=True), axis=1, keepdims=True)
+
+    fold_gram = [
+        [jnp.sum(fold_rows[e : e + 1] * fold_rows[k : k + 1], axis=1, keepdims=True) for k in range(n_tp)]
+        for e in range(n_tp)
+    ]
+    crossed = dot_halves(halves(fold_rows), halves(prior[...]))
+    crossed = [
+        jnp.concatenate(
+            [crossed[e : e + 1, tile * LANES : (tile + 1) * LANES] for tile in range(n_dp)], axis=0
+        )
+        for e in range(n_tp)
+    ]
+    prior_square = jnp.zeros((rows, LANES), f32)
+    for tile in range(n_dp):
+        part = prior[:, tile * LANES : (tile + 1) * LANES]
+        prior_square = prior_square + part * part
+    prior_mass = total(prior_square)
 
     received(SIDE, zrecv)
     sides = jnp.concatenate(
@@ -351,19 +369,15 @@
         first = [jnp.where(flip, b, a) for a, b in zip(lower, upper)]
         return first, [jnp.where(flip, a, b) for a, b in zip(lower, upper)]
 
-    def total(value):
-        return jnp.sum(jnp.sum(value, axis=0, keepdims=True), axis=1, keepdims=True)
-
     received(SLICE, grads.at[: n_tp - 1])
-    leaf_square = jnp.zeros((rows, LANES), f32)
-    for tile in range(n_dp):
-        leaf = prior[:, tile * LANES : (tile + 1) * LANES]
-        for e in range(n_tp):
-            step = grads[e, tile : tile + 1, :]
-            grads_out[e : e + 1, tile * LANES : (tile + 1) * LANES] = step
-            leaf = leaf + fold[:, e : e + 1] * step
-        leaf_square = leaf_square + leaf * leaf
-    own_mass = total(leaf_square)
+    steps = [grads[e] for e in range(n_tp)]
+    growth = jnp.zeros((n_dp, LANES), f32)
+    for e, step in enumerate(steps):
+        slope = 2.0 * crossed[e]
+        for other, weight in zip(steps, fold_gram[e]):
+            slope = slope + weight * other
+        growth = growth + step * slope
+    own_mass = prior_mass + total(growth)
 
     received(NODE, node_recv.at[: half - 1])
     mixtures = [[[node_recv[j]] for j in range(half)]]
@@ -444,6 +458,9 @@
         packed = jnp.where(lane == n_dp + index, value, packed)
     sums_all[slot] = packed
     exchange_all(SUM, lambda d, t: sums_all.at[slot], sums_all.at[slot])
+    for e, step in enumerate(steps):
+        for tile in range(n_dp):
+            grads_out[e : e + 1, tile * LANES : (tile + 1) * LANES] = step[tile : tile + 1]
     received(PEER, peer_all)
     received(MIX, mix_recv)
     steps_of, peer_every = steps_from(peer_all)

time: 39.5 us -> 39.2 us (level)
  no operation moved by 1% of the time
where the time goes in v9:
time: 39.2 us; the launch traced here: 39 us
  Pallas kernels  37.7 us (96%)
  between operations  1.29 us (3%)
    pallas_call x1, Pallas kernels, fused_body(): pl.pallas_call(functools.partial(fused_kernel, n_dp, n_tp), out_shape=(ja...  36.7 us
    pallas_call x1, Pallas kernels, fused_body(): pl.pallas_call(last_kernel, out_shape=(jax.ShapeDtypeStruct((rows, column...  0.99 us

profile of v9, /device:TPU:0, one launch (start us, length us, event | category | flops | bytes accessed | tf_op | source)
XLA Modules:
  0.0 39.0 jit_solution(2208072932164474502)
XLA Ops:
  1.3 36.7 %shard_map.104 = (f32[256,1024]{1,0:T(8,128)S(1)}, f32[4,256]{1,0:T(4,128)S(1)}, f32[4,1024]{1,0:T(4,128)S(1)}) custom-call(bf16[512,2048]{1,0:T(8,128)(2,1)} %act_hbm.1, bf16[512,7168]{1,0:T(8,128)(2,1)} %out_hbm.1, bf16[64,2048]{1,0:T(8,128)(2,1)} %bitcast.5, bf16[64,7168]{1,0:T(8,128)(2,1)} %bitcast.4, s32[1]{0:T(128)S(6)} %copy.11.count_ref, ...), custom_call_target="tpu_custom_call" | custom-call | tf_op jit(solution)/shard_map/pallas_call | solution.py:639
  38.0 1.0 %shard_map.105 = (f32[256,1024]{1,0:T(8,128)}, f32[4,1024]{1,0:T(4,128)}) custom-call(f32[256,1024]{1,0:T(8,128)S(1)} %get-tuple-element.5.root_ref, f32[4,256]{1,0:T(4,128)S(1)} %get-tuple-element.6.solved_ref, f32[4,1024]{1,0:T(4,128)S(1)} %get-tuple-element.7.grads_ref), custom_call_target="tpu_custom_call" | custom-call | tf_op jit(solution)/shard_map/pallas_call | solution.py:695

commit v10 on v9

--- a/solution.py
+++ b/solution.py
@@ -230,16 +230,19 @@
     def received(phase, ref):
         drain(ref, sems.at[1, phase])
 
+    z_peers = (diagonal, far, near)
+    dp_peers = [2 * other + side for other in (chip_d, chip_x, chip_y) for side in (core, 1 - core)]
+    dp_peers.append(partner)
+
     def exchange(axis, phase, source, target):
-        size, other = (n_tp, tp_of) if axis == "tensor" else (n_dp, dp_of)
-        for k in range(1, size):
-            push(phase, source(other(k)), target, **{axis: other(k)})
+        for other in z_peers if axis == "tensor" else dp_peers:
+            push(phase, source(other), target, **{axis: other})
 
     def exchange_all(phase, source, target):
-        for j in sorted(range(n_tp), key=lambda j: -min(j, n_tp - j)):
-            for k in range(n_dp):
-                if (j, k) != (0, 0):
-                    push(phase, source(dp_of(k), tp_of(j)), target, dp=dp_of(k), tensor=tp_of(j))
+        for t in (*z_peers, z):
+            for d in (*dp_peers, me):
+                if t is not z or d is not me:
+                    push(phase, source(d, t), target, dp=d, tensor=t)
 
     def sides_of_rows(index, start, count):
         spans = [slice(start + h * count, start + (h + 1) * count) for h in range(2)]

time: 39.2 us -> 39.1 us (level)
  no operation moved by 1% of the time
where the time goes in v10:
time: 39.1 us; the launch traced here: 39 us
  Pallas kernels  37.7 us (96%)
  between operations  1.29 us (3%)
    pallas_call x1, Pallas kernels, fused_body(): pl.pallas_call(functools.partial(fused_kernel, n_dp, n_tp), out_shape=(ja...  36.7 us
    pallas_call x1, Pallas kernels, fused_body(): pl.pallas_call(last_kernel, out_shape=(jax.ShapeDtypeStruct((rows, column...  0.99 us

profile of v10, /device:TPU:0, one launch (start us, length us, event | category | flops | bytes accessed | tf_op | source)
XLA Modules:
  0.0 39.0 jit_solution(11670701693705600139)
XLA Ops:
  1.3 36.7 %shard_map.104 = (f32[256,1024]{1,0:T(8,128)S(1)}, f32[4,256]{1,0:T(4,128)S(1)}, f32[4,1024]{1,0:T(4,128)S(1)}) custom-call(bf16[512,2048]{1,0:T(8,128)(2,1)} %act_hbm.1, bf16[512,7168]{1,0:T(8,128)(2,1)} %out_hbm.1, bf16[64,2048]{1,0:T(8,128)(2,1)} %bitcast.5, bf16[64,7168]{1,0:T(8,128)(2,1)} %bitcast.4, s32[1]{0:T(128)S(6)} %copy.11.count_ref, ...), custom_call_target="tpu_custom_call" | custom-call | tf_op jit(solution)/shard_map/pallas_call | solution.py:642
  38.0 1.0 %shard_map.105 = (f32[256,1024]{1,0:T(8,128)}, f32[4,1024]{1,0:T(4,128)}) custom-call(f32[256,1024]{1,0:T(8,128)S(1)} %get-tuple-element.5.root_ref, f32[4,256]{1,0:T(4,128)S(1)} %get-tuple-element.6.solved_ref, f32[4,1024]{1,0:T(4,128)S(1)} %get-tuple-element.7.grads_ref), custom_call_target="tpu_custom_call" | custom-call | tf_op jit(solution)/shard_map/pallas_call | solution.py:698

commit v11 on v10

--- a/solution.py
+++ b/solution.py
@@ -345,9 +345,9 @@
     )
     lane = lax.broadcasted_iota(jnp.int32, sides.shape, 1)
     doubled = jnp.where(lane < RANK, sides, pltpu.roll(sides, RANK, 1))
-    product = dot_mid(sides.T, doubled) / jnp.sqrt(f32(SEQ))
+    product = dot_mid(sides.T[RANK:], doubled) / jnp.sqrt(f32(SEQ))
     product = jnp.where(z < count_ref[0], product, jnp.zeros_like(product))
-    full[...] = product[RANK:]
+    full[...] = product
     even = full[pl.ds(0, RANK // 2, stride=2), :]
     odd = full[pl.ds(1, RANK // 2, stride=2), :]
     lane = lax.broadcasted_iota(jnp.int32, even.shape, 1)
@@ -513,13 +513,16 @@
 
     chunk_halves = halves(jnp.concatenate(chunks, axis=1))
     upper_halves, lower_halves = [[v[s] for v in chunk_halves] for s in (slice(0, LANES), slice(LANES, rows))]
-    targets = dot_flip_halves(every_halves, chunk_halves)
+    below = dot_flip_halves(
+        [jnp.concatenate(pair, axis=0) for pair in zip(lower_halves, every_halves)], chunk_halves
+    )
+    targets = below[LANES:]
     unit = rows / trace
     triangle = jnp.concatenate(
         [
             dot_flip_halves(upper_halves, upper_halves),
-            dot_flip_halves(lower_halves, upper_halves),
-            dot_flip_halves(lower_halves, lower_halves),
+            below[:LANES, :LANES],
+            below[:LANES, LANES:],
         ],
         axis=0,
     )

time: 39.1 us -> 39 us (level)
  no operation moved by 1% of the time
where the time goes in v11:
time: 39 us; the launch traced here: 38.9 us
  Pallas kernels  37.6 us (96%)
  between operations  1.29 us (3%)
    pallas_call x1, Pallas kernels, fused_body(): pl.pallas_call(functools.partial(fused_kernel, n_dp, n_tp), out_shape=(ja...  36.6 us
    pallas_call x1, Pallas kernels, fused_body(): pl.pallas_call(last_kernel, out_shape=(jax.ShapeDtypeStruct((rows, column...  0.99 us

profile of v11, /device:TPU:0, one launch (start us, length us, event | category | flops | bytes accessed | tf_op | source)
XLA Modules:
  0.0 38.9 jit_solution(14641335159477763916)
XLA Ops:
  1.3 36.6 %shard_map.104 = (f32[256,1024]{1,0:T(8,128)S(1)}, f32[4,256]{1,0:T(4,128)S(1)}, f32[4,1024]{1,0:T(4,128)S(1)}) custom-call(bf16[512,2048]{1,0:T(8,128)(2,1)} %act_hbm.1, bf16[512,7168]{1,0:T(8,128)(2,1)} %out_hbm.1, bf16[64,2048]{1,0:T(8,128)(2,1)} %bitcast.5, bf16[64,7168]{1,0:T(8,128)(2,1)} %bitcast.4, s32[1]{0:T(128)S(6)} %copy.11.count_ref, ...), custom_call_target="tpu_custom_call" | custom-call | tf_op jit(solution)/shard_map/pallas_call | solution.py:645
  37.9 1.0 %shard_map.105 = (f32[256,1024]{1,0:T(8,128)}, f32[4,1024]{1,0:T(4,128)}) custom-call(f32[256,1024]{1,0:T(8,128)S(1)} %get-tuple-element.5.root_ref, f32[4,256]{1,0:T(4,128)S(1)} %get-tuple-element.6.solved_ref, f32[4,1024]{1,0:T(4,128)S(1)} %get-tuple-element.7.grads_ref), custom_call_target="tpu_custom_call" | custom-call | tf_op jit(solution)/shard_map/pallas_call | solution.py:701

commit v12 on v11

--- a/solution.py
+++ b/solution.py
@@ -152,8 +152,10 @@
     gram_rs,
     gram_z,
     gram_all,
+    sent,
     load_sem,
     sems,
+    send_sems,
     root_sems,
     out_sem,
     ready_sem,
@@ -221,14 +223,14 @@
         pltpu.make_async_remote_copy(
             src_ref=source,
             dst_ref=target,
-            send_sem=sems.at[0, phase],
-            recv_sem=sems.at[1, phase],
+            send_sem=send_sems.at[{SCATTER: 1, GATHER: 2}.get(phase, 0)],
+            recv_sem=sems.at[phase],
             device_id=device,
             device_id_type=MESH,
         ).start()
 
     def received(phase, ref):
-        drain(ref, sems.at[1, phase])
+        drain(ref, sems.at[phase])
 
     z_peers = (diagonal, far, near)
     dp_peers = [2 * other + side for other in (chip_d, chip_x, chip_y) for side in (core, 1 - core)]
@@ -551,7 +553,7 @@
     def relayed(index, count):
         drain(root.at[:, : count * LANES] if count else root.at[upper, :LANES], root_sems.at[index])
 
-    drain(gram_rs.at[: half - 1], sems.at[0, SCATTER])
+    drain(gram_rs.at[: half - 1], send_sems.at[1])
     relay(0, me, dev_x)
     relay(1, me, dev_y)
     received(SCATTER, gram_rs.at[: half - 1])
@@ -576,19 +578,7 @@
     relayed(2, 0)
     relayed(3, 0)
     relay(4, dev_d, partner)
-    for phase, ref in (
-        (PAIR, pair_in),
-        (NODE, node_recv.at[: half - 1]),
-        (MID, zmid),
-        (SIDE, zrecv),
-        (SLICE, grads.at[: n_tp - 1]),
-        (ROW, grads_all.at[: n_tp * n_dp - 1]),
-        (SUM, sums_all.at[: n_tp * n_dp - 1]),
-        (PEER, peer_all),
-        (MIX, mix_recv),
-        (ALONG, gram_z.at[: n_tp - 1]),
-    ):
-        drain(ref, sems.at[0, phase])
+    drain(sent, send_sems.at[0])
     received(GATHER, gram_all.at[: n_dp - 1])
     triangle = jnp.concatenate([gram_all[r] for r in range(n_dp)], axis=0)
     corner = triangle[LANES:rows]
@@ -600,7 +590,7 @@
         axis=0,
     )
     solved_out[...] = solve(gram, target)
-    drain(gram_all.at[: n_dp - 1], sems.at[0, GATHER])
+    drain(gram_all.at[: n_dp - 1], send_sems.at[2])
     relayed(4, half - 1)
     root_write = pltpu.make_async_copy(root, root_out, out_sem.at[0])
     root_write.start()
@@ -641,6 +631,8 @@
     devices = n_dp * n_tp
     own_rows = 3 * LANES // n_dp
     part_rows = own_rows + 2 * slots
+    whole = (3 * (n_dp // 2) - 1) * rows + 3 * SEQ
+    sent_rows = whole + (n_tp - 1) * (n_dp + part_rows) + 3 * devices - 2
     pin = functools.partial(pltpu.with_memory_space_constraint, memory_space=pltpu.HBM)
     root, solved, grads = pl.pallas_call(
         functools.partial(fused_kernel, n_dp, n_tp),
@@ -678,8 +670,10 @@
             pltpu.VMEM((n_dp // 2, part_rows, LANES), f32),
             pltpu.VMEM((n_tp, part_rows, LANES), f32),
             pltpu.VMEM((n_dp, own_rows, LANES), f32),
+            pltpu.VMEM((sent_rows, 1, LANES), f32),
             pltpu.SemaphoreType.DMA((10,)),
-            pltpu.SemaphoreType.DMA((2, 12)),
+            pltpu.SemaphoreType.DMA((12,)),
+            pltpu.SemaphoreType.DMA((3,)),
             pltpu.SemaphoreType.DMA((6,)),
             pltpu.SemaphoreType.DMA((1,)),
             pltpu.SemaphoreType.REGULAR,

time: 39 us -> 39 us (level)
  no operation moved by 1% of the time
where the time goes in v12:
time: 39 us; the launch traced here: 38.8 us
  Pallas kernels  37.5 us (96%)
  between operations  1.29 us (3%)
    pallas_call x1, Pallas kernels, fused_body(): pl.pallas_call(functools.partial(fused_kernel, n_dp, n_tp), out_shape=(ja...  36.5 us
    pallas_call x1, Pallas kernels, fused_body(): pl.pallas_call(last_kernel, out_shape=(jax.ShapeDtypeStruct((rows, column...  0.99 us

profile of v12, /device:TPU:0, one launch (start us, length us, event | category | flops | bytes accessed | tf_op | source)
XLA Modules:
  0.0 38.8 jit_solution(4345463551970729366)
XLA Ops:
  1.3 36.5 %shard_map.104 = (f32[256,1024]{1,0:T(8,128)S(1)}, f32[4,256]{1,0:T(4,128)S(1)}, f32[4,1024]{1,0:T(4,128)S(1)}) custom-call(bf16[512,2048]{1,0:T(8,128)(2,1)} %act_hbm.1, bf16[512,7168]{1,0:T(8,128)(2,1)} %out_hbm.1, bf16[64,2048]{1,0:T(8,128)(2,1)} %bitcast.5, bf16[64,7168]{1,0:T(8,128)(2,1)} %bitcast.4, s32[1]{0:T(128)S(6)} %copy.11.count_ref, ...), custom_call_target="tpu_custom_call" | custom-call | tf_op jit(solution)/shard_map/pallas_call | solution.py:637
  37.8 1.0 %shard_map.105 = (f32[256,1024]{1,0:T(8,128)}, f32[4,1024]{1,0:T(4,128)}) custom-call(f32[256,1024]{1,0:T(8,128)S(1)} %get-tuple-element.5.root_ref, f32[4,256]{1,0:T(4,128)S(1)} %get-tuple-element.6.solved_ref, f32[4,1024]{1,0:T(4,128)S(1)} %get-tuple-element.7.grads_ref), custom_call_target="tpu_custom_call" | custom-call | tf_op jit(solution)/shard_map/pallas_call | solution.py:695
